TPU v7x, 128 devices: a whole 4x4x4 slice. The times are simulated.
128 devices in a mesh: snp: 16 (over z_lo, y, core), samp: 8 (over x, z_hi).
Axes of the slice: x: 4, y: 4, z: 4 (z_hi: 2, z_lo: 2; z = z_hi * 2 + z_lo), core: 2. Of those that a mesh axis runs over, the one named last changes fastest.
Arguments:
- genotypes: float32 [16384, 4096], P('snp', 'samp'), may hold values from -1 to 2, as said below
- pcs: float32 [20, 4096], P(None, 'samp'), may hold values from -6 to 6
Outputs:
- kinship: float32 [4096, 4096], P('snp', 'samp')
Inputs may be any that keep to these rules, and one draw needn't show every extreme that they name: `genotypes`: observed entries are real-valued dosages from 0 to 2 and -1 marks a missing entry; SNPs whose index is a multiple of 16 are never missing.
All inputs are finite; a program needn't handle non-finite values.
Results may differ from a plain program's by a relative error of at most 0.0015.
Values may be sent and summed in bfloat16 or wider, within the bound.
A program may use at most 64 MiB of HBM per device.

v0:
```python
import functools

import jax
import jax.numpy as jnp
from jax import lax
from jax.experimental import pallas as pl
from jax.experimental.pallas import tpu as pltpu
from jax.sharding import PartitionSpec as P

AXES = ("snp", "samp")
HIGH = lax.Precision.HIGHEST
MISSING = 4.0
PAD = 32
TILE = 256


def decode(snp, samp):
    return samp // 2, (snp // 2) % 4, samp % 2, snp // 8, snp % 2


def encode(x, y, zh, zl, c):
    return ((zl * 4 + y) * 2 + c) * 8 + x * 2 + zh


def pairs(where):
    return [(s * 8 + j, encode(*where(*decode(s, j)))) for s in range(16) for j in range(8)]


def move(value, where):
    return lax.ppermute(value, AXES, pairs(where))


def from_x(value, d):
    return move(value, lambda x, y, zh, zl, c: ((x - d) % 4, y, zh, zl, c))


def from_z(value, d):
    def where(x, y, zh, zl, c):
        z = (zh * 2 + zl - d) % 4
        return x, y, z // 2, z % 2, c

    return move(value, where)


def flip(value):
    return move(value, lambda x, y, zh, zl, c: (x, y, zh, zl, 1 - c))


def from_y(value, d):
    return move(value, lambda x, y, zh, zl, c: (x, (y - d) % 4, zh, zl, c))


def rows_at(y, zh):
    return zh * ((y % 2) * 2 + y // 2) + (1 - zh) * (y ^ (y // 2))


def to_owner(value):
    def where(x, y, zh, zl, c):
        xi = rows_at(y, zh)
        return x, (xi % 2) * 2 + zh, c, xi // 2, zl

    return move(value, where)


LEFT = (0, 0, 1, 0, 2, 1)
RIGHT = (0, 1, 0, 2, 0, 1)


def terms_kernel(order, value, out):
    a = value[...]
    parts = []
    for _ in range(3):
        parts.append(a.astype(jnp.bfloat16))
        a = a - parts[-1].astype(jnp.float32)
    for k, part in enumerate(order):
        out[k * PAD : (k + 1) * PAD, :] = parts[part]


def terms(value, order):
    rows, columns = value.shape
    return pl.pallas_call(
        functools.partial(terms_kernel, order),
        out_shape=jax.ShapeDtypeStruct((rows * len(order), columns), jnp.bfloat16),
        compiler_params=pltpu.CompilerParams(vmem_limit_bytes=4 << 20),
        name="terms",
    )(value)


def frequencies(coef6, design6):
    fitted = lax.dot_general(coef6, design6, (((0,), (0,)), ((), ())), preferred_element_type=jnp.float32)
    return jnp.clip(0.5 * fitted, 0.02, 0.98)


def spread_kernel(left, right, out):
    @pl.loop(0, right.shape[1] // TILE)
    def _(k):
        at = pl.ds(pl.multiple_of(k * TILE, TILE), TILE)
        freq = frequencies(left[...], right[:, at])
        out[:, at] = jnp.sqrt(freq * (1.0 - freq)).astype(jnp.bfloat16)


def spreads(left, right):
    rows, columns = left.shape[1], right.shape[1]
    return pl.pallas_call(
        spread_kernel,
        grid=(rows // TILE,),
        in_specs=[
            pl.BlockSpec((left.shape[0], TILE), lambda i: (0, i)),
            pl.BlockSpec(right.shape, lambda i: (0, 0)),
        ],
        out_specs=pl.BlockSpec((TILE, columns), lambda i: (i, 0)),
        out_shape=jax.ShapeDtypeStruct((rows, columns), jnp.bfloat16),
        compiler_params=pltpu.CompilerParams(vmem_limit_bytes=12 << 20),
        name="spreads",
    )(left, right)


def open_kernel(code, raw, resid, spread):
    seen = code[...] < 3.0
    resid[...] = jnp.where(seen, code[...], jnp.zeros_like(code))
    spread[...] = jnp.where(seen, raw[...], jnp.zeros_like(code))


def open_code(code, raw, which):
    rows, columns = code.shape
    block = pl.BlockSpec((TILE, columns), lambda i: (i, 0))
    return pl.pallas_call(
        open_kernel,
        grid=(rows // TILE,),
        in_specs=[block, pl.BlockSpec((TILE, columns), lambda i: (i, which))],
        out_specs=[block, block],
        out_shape=[jax.ShapeDtypeStruct(code.shape, jnp.bfloat16)] * 2,
        compiler_params=pltpu.CompilerParams(vmem_limit_bytes=8 << 20),
        name="open_code",
    )(code, raw)


def gram(a, b):
    return lax.dot_general(a, b, (((0,), (0,)), ((), ())), preferred_element_type=jnp.float32)


def body(genotypes, pcs):
    x, y, zh, zl, c = decode(lax.axis_index("snp"), lax.axis_index("samp"))
    here = genotypes.shape[1]
    half = here // 2
    count = pcs.shape[0] + 1
    design = jnp.concatenate([jnp.ones((1, here), jnp.float32), pcs, jnp.zeros((PAD - count, here), jnp.float32)], axis=0)
    design_zh = jnp.stack([design, from_z(design, 2)])
    designs = [design_zh] + [from_x(design_zh, d) for d in (1, 2, 3)]
    observed = genotypes >= 0.0
    dosage = jnp.where(observed, genotypes, 0.0)
    cross = lax.dot_general(design, dosage, (((1,), (1,)), ((), ())), precision=HIGH)
    cross = cross + from_z(cross, 2)
    cross = (cross + from_x(cross, 2)) + (from_x(cross, 1) + from_x(cross, 3))
    total = None
    for d in designs:
        for k in range(2):
            part = lax.dot_general(d[k], d[k], (((1,), (1,)), ((), ())), precision=HIGH)
            total = part if total is None else total + part
    factor = jnp.linalg.cholesky(total[:count, :count])
    inverse = jax.scipy.linalg.cho_solve((factor, True), jnp.eye(count, dtype=jnp.float32))
    inverse = jnp.pad(inverse, ((0, PAD - count), (0, PAD - count)))
    coef = jnp.dot(inverse, cross, precision=HIGH)
    coef_far = from_z(coef, 1)

    def in_order(a, b):
        return jnp.concatenate([jnp.where(zh == 0, a, b), jnp.where(zh == 0, b, a)], axis=1)

    def my_half(value):
        return lax.dynamic_slice(value, (0, zl * half), (value.shape[0], half))

    own6 = terms(design, RIGHT)
    all6 = terms(jnp.concatenate([in_order(*designs[0])] + [my_half(d[0]) for d in designs], axis=1), RIGHT)
    near6 = terms(coef, LEFT)
    freq = frequencies(near6, own6)
    code = jnp.where(observed, dosage - 2.0 * freq, MISSING).astype(jnp.bfloat16)
    code, coef_far = lax.optimization_barrier((code, coef_far))
    up, down = from_z(code, 1), from_z(code, 3)
    near_half = my_half(code)
    near_rows = [near_half] + [from_x(near_half, d) for d in (1, 2, 3)]
    raw = spreads(jnp.concatenate([near6, terms(coef_far, LEFT)], axis=1), all6)
    far_same = jnp.where(zl == 0, up, down)
    far_other = jnp.where(zl == 0, down, up)
    far_half = my_half(far_same)
    far_rows = [far_half] + [from_x(far_half, d) for d in (1, 2, 3)]
    across = from_z(lax.optimization_barrier((code, up, down))[0], 2)
    rows = jnp.concatenate([jnp.concatenate(near_rows, axis=1), jnp.concatenate(far_rows, axis=1)], axis=0)
    row_resid, row_spread = open_code(rows, raw, 1)
    columns = jnp.concatenate([in_order(code, across), in_order(far_same, far_other)], axis=0)
    col_resid, col_spread = open_code(columns, raw, 0)

    sums = None
    for step in (2, 1, 3, 0):
        at = (0, (rows_at((y + step) % 4, zh) - x) % 4 * half)
        numer = gram(lax.dynamic_slice(row_resid, at, (rows.shape[0], half)), col_resid)
        denom = gram(lax.dynamic_slice(row_spread, at, (rows.shape[0], half)), col_spread)
        both = jnp.stack([numer, denom])
        keep = lax.dynamic_slice(both, (0, 0, c * here), (2, half, here))
        give = lax.dynamic_slice(both, (0, 0, (1 - c) * here), (2, half, here))
        merged = keep + flip(give)
        if step:
            low = merged[1].astype(jnp.bfloat16)
            top = merged[0] * (low.astype(jnp.float32) / merged[1])
            merged = from_y(jnp.stack([top.astype(jnp.bfloat16), low]), 4 - step).astype(jnp.float32)
        sums = merged if sums is None else sums + merged
    return to_owner(sums[0] / (4.0 * sums[1]))


def solution(mesh):
    in_specs = (P("snp", "samp"), P(None, "samp"))
    out_specs = P("snp", "samp")
    return jax.shard_map(body, mesh=mesh, in_specs=in_specs, out_specs=out_specs, check_vma=False)
```

profile of v0, /device:TPU:32, one launch (start us, length us, event | category | flops | bytes accessed | tf_op | source)
XLA Modules:
  0.0 183.7 jit_solution(3115951260503879598)
XLA Ops:
  0.1 1.0 maximum_maximum_fusion.2.value
  1.1 3.1 %collective-permute-start = (f32[32,512]{1,0:T(8,128)S(1)}, f32[32,512]{1,0:T(8,128)S(1)}, u32[]{:S(2)}, u32[]{:S(2)}) collective-permute-start(f32[32,512]{1,0:T(8,128)S(1)} %maximum_maximum_fusion.2.value), channel_id=1, source_target_pairs={{0,1},{1,0},{2,3},{3,2},{4,5},{5,4},{6,7},{7,6},{8,9},{9,8},{10,11... | collective-permute-start | bytes 196616 | tf_op jit(solution)/shard_map/ppermute | solution.py:30
  4.2 3.6 %fusion.1 = f32[32,1024]{1,0:T(8,128)S(1)} fusion(f32[1024,512]{1,0:T(8,128)} %param.2, f32[20,512]{1,0:T(8,128)} %param.3, f32[32]{0:T(128)S(1)} %pad.37.clone, f32[32]{0:T(128)S(1)} %pad.35.clone), kind=kOutput, calls=%fused_computation.21 | convolution fusion | flops 202407936 | bytes 2269440 | tf_op jit(solution)/shard_map/dot_general | solution.py:152
  7.8 0.6 collective-permute-start.4
  8.4 1.1 fusion.63
  9.6 0.9 select_dynamic-update-slice_fusion.1
  10.5 0.9 select_dynamic-update-slice_fusion
  11.4 1.6 collective-permute-start.3
  13.0 2.7 %collective-permute-start.2 = (f32[2,32,512]{2,1,0:T(8,128)S(1)}, f32[2,32,512]{2,1,0:T(8,128)S(1)}, u32[]{:S(2)}, u32[]{:S(2)}) collective-permute-start(f32[2,32,512]{2,1,0:T(8,128)S(1)} %pad_maximum_fusion.4), channel_id=1, source_target_pairs={{0,4},{1,5},{2,6},{3,7},{4,0},{5,1},{6,2},{7,3},{8,12},{9,13},{10,... | collective-permute-start | bytes 393224 | tf_op jit(solution)/shard_map/ppermute | solution.py:30
  15.7 1.4 collective-permute-start.1
  17.4 0.7 collective-permute-start.7
  18.0 2.6 %collective-permute-start.6 = (f32[32,1024]{1,0:T(8,128)S(1)}, f32[32,1024]{1,0:T(8,128)S(1)}, u32[]{:S(2)}, u32[]{:S(2)}) collective-permute-start(f32[32,1024]{1,0:T(8,128)S(1)} %add.201), channel_id=1, source_target_pairs={{0,6},{1,7},{2,0},{3,1},{4,2},{5,3},{6,4},{7,5},{8,14},{9,15},{10,... | collective-permute-start | bytes 393224 | tf_op jit(solution)/shard_map/ppermute | solution.py:30
  20.7 1.0 collective-permute-start.5
  22.1 0.4 collective-permute-done.2
  23.5 1.9 %cholesky.17 = f32[21,21]{1,0:T(8,128)S(1)} custom-call(f32[21,21]{1,0:T(8,128)S(1)} %fusion.48), custom_call_target="Cholesky" | custom-call | tf_op jit(solution)/shard_map/jit(cholesky)/cholesky | solution.py:160
  25.4 0.6 compare_reduce_fusion
  26.1 0.6 fusion.43
  26.8 1.6 custom-call.10
  28.4 0.2 fusion.46
  28.8 1.2 fusion.29.value
  29.9 0.8 collective-permute-start.8
  30.8 1.8 fusion
  32.6 2.4 %collective-permute-done.8.value = f32[32,1024]{1,0:T(8,128)S(1)} collective-permute-done((f32[32,1024]{1,0:T(8,128)S(1)}, f32[32,1024]{1,0:T(8,128)S(1)}, u32[]{:S(2)}, u32[]{:S(2)}) %collective-permute-start.8) | collective-permute-done | bytes 131104 | tf_op jit(solution)/shard_map/ppermute | solution.py:30
  35.0 1.9 %collective-permute-start.13 = (bf16[1024,512]{1,0:T(8,128)(2,1)}, bf16[1024,512]{1,0:T(8,128)(2,1)S(1)}, u32[]{:S(2)}, u32[]{:S(2)}) collective-permute-start(bf16[1024,512]{1,0:T(8,128)(2,1)} %fusion), channel_id=1, source_target_pairs={{0,64},{1,65},{2,66},{3,67},{4,68},{5,69},{6,70},{7,71},{8,72},{9,... | collective-permute-start | bytes 3145736 | tf_op jit(solution)/shard_map/ppermute | solution.py:30
  37.1 1.1 constant_dynamic-slice_fusion.1
  38.2 0.4 collective-permute-start.11
  38.7 3.2 %collective-permute-start.10 = (bf16[1024,256]{1,0:T(8,128)(2,1)S(1)}, bf16[1024,256]{1,0:T(8,128)(2,1)S(1)}, u32[]{:S(2)}, u32[]{:S(2)}) collective-permute-start(bf16[1024,256]{1,0:T(8,128)(2,1)S(1)} %constant_dynamic-slice_fusion.1), channel_id=1, source_target_pairs={{0,4},{1,5},{2,6},{3,7},{4,0},{5,1},{6,2},{7,3},{8,12},{9,13},{10,... | collective-permute-start | bytes 1572872 | tf_op jit(solution)/shard_map/ppermute | solution.py:30
  41.9 1.9 %collective-permute-start.9 = (bf16[1024,256]{1,0:T(8,128)(2,1)S(1)}, bf16[1024,256]{1,0:T(8,128)(2,1)S(1)}, u32[]{:S(2)}, u32[]{:S(2)}) collective-permute-start(bf16[1024,256]{1,0:T(8,128)(2,1)S(1)} %constant_dynamic-slice_fusion.1), channel_id=1, source_target_pairs={{0,6},{1,7},{2,0},{3,1},{4,2},{5,3},{6,4},{7,5},{8,14},{9,15},{10,... | collective-permute-start | bytes 1572872 | tf_op jit(solution)/shard_map/ppermute | solution.py:30
  43.8 12.2 %collective-permute-done.13 = bf16[1024,512]{1,0:T(8,128)(2,1)S(1)} collective-permute-done((bf16[1024,512]{1,0:T(8,128)(2,1)}, bf16[1024,512]{1,0:T(8,128)(2,1)S(1)}, u32[]{:S(2)}, u32[]{:S(2)}) %collective-permute-start.13) | collective-permute-done | bytes 1048608 | tf_op jit(solution)/shard_map/ppermute | solution.py:30
  56.1 2.5 %collective-permute-done.12 = bf16[1024,512]{1,0:T(8,128)(2,1)S(1)} collective-permute-done((bf16[1024,512]{1,0:T(8,128)(2,1)}, bf16[1024,512]{1,0:T(8,128)(2,1)S(1)}, u32[]{:S(2)}, u32[]{:S(2)}) %collective-permute-start.12) | collective-permute-done | bytes 1048608 | tf_op jit(solution)/shard_map/ppermute | solution.py:30
  58.6 1.1 broadcast_select_fusion.1
  59.7 1.4 collective-permute-start.16
  61.2 3.2 %collective-permute-start.15 = (bf16[1024,256]{1,0:T(8,128)(2,1)S(1)}, bf16[1024,256]{1,0:T(8,128)(2,1)S(1)}, u32[]{:S(2)}, u32[]{:S(2)}) collective-permute-start(bf16[1024,256]{1,0:T(8,128)(2,1)S(1)} %constant_dynamic-slice_fusion), channel_id=1, source_target_pairs={{0,4},{1,5},{2,6},{3,7},{4,0},{5,1},{6,2},{7,3},{8,12},{9,13},{10,... | collective-permute-start | bytes 1572872 | tf_op jit(solution)/shard_map/ppermute | solution.py:30
  64.4 1.0 collective-permute-start.14
  65.4 19.9 %spreads.1.raw = bf16[2048,2048]{1,0:T(8,128)(2,1)S(1)} custom-call(bf16[192,2048]{1,0:T(8,128)(2,1)S(1)} %pad_maximum_fusion.left, bf16[192,2048]{1,0:T(8,128)(2,1)S(1)} %terms.7.right), custom_call_target="tpu_custom_call" | custom-call | tf_op jit(solution)/shard_map/spreads/pallas_call | solution.py:104
  85.4 3.1 %collective-permute-start.17 = (bf16[1024,512]{1,0:T(8,128)(2,1)}, bf16[1024,512]{1,0:T(8,128)(2,1)S(1)}, u32[]{:S(2)}, u32[]{:S(2)}) collective-permute-start(bf16[1024,512]{1,0:T(8,128)(2,1)} %fusion), channel_id=1, source_target_pairs={{0,1},{1,0},{2,3},{3,2},{4,5},{5,4},{6,7},{7,6},{8,9},{9,8},{10,11... | collective-permute-start | bytes 3145736 | tf_op jit(solution)/shard_map/ppermute | solution.py:30
  88.5 1.2 broadcast_select_fusion
  89.8 23.5 %maximum_maximum_fusion.code = bf16[2048,1024]{1,0:T(8,128)(2,1)S(1)} fusion(bf16[1024,256]{1,0:T(8,128)(2,1)S(1)} %collective-permute-done.16, bf16[1024,256]{1,0:T(8,128)(2,1)S(1)} %collective-permute-done.15, bf16[1024,256]{1,0:T(8,128)(2,1)S(1)} %collective-permute-done.14, bf16[1024,256]{1,0:T(8,128)(2,1)S(1)} %constant_dynamic-slice_fusion, ...), kind=kLoop, calls=%fused_computation | loop fusion | flops 33554432 | bytes 8388608 | tf_op jit(solution)/shard_map/concatenate | solution.py:187
  113.3 1.4 open_code.2
  114.8 2.7 %broadcast_select_fusion.3 = (bf16[1024,512]{1,0:T(8,128)(2,1)}, bf16[1024,512]{1,0:T(8,128)(2,1)}) fusion(bf16[1024,512]{1,0:T(8,128)(2,1)} %fusion, bf16[1024,512]{1,0:T(8,128)(2,1)S(1)} %collective-permute-done.17, pred[]{:T(512)S(6)} %eq.30), kind=kLoop, calls=%fused_computation.56 | loop fusion | flops 1048576 | bytes 4194305 | tf_op jit(solution)/shard_map/jit(_where)/select_n | solution.py:167
  117.5 2.7 %maximum_maximum_fusion.1.code = bf16[2048,1024]{1,0:T(8,128)(2,1)S(1)} fusion(bf16[1024,512]{1,0:T(8,128)(2,1)} %broadcast_select_fusion, bf16[1024,512]{1,0:T(8,128)(2,1)} %get-tuple-element.25, bf16[1024,512]{1,0:T(8,128)(2,1)} %get-tuple-element.28, bf16[1024,512]{1,0:T(8,128)(2,1)} %get-tuple-element.27), kind=kLoop, calls=%fused_computation.1 | loop fusion | flops 16777216 | bytes 8388608 | tf_op jit(solution)/shard_map/concatenate | solution.py:189
  120.2 1.7 open_code.3
  121.9 1.3 convolution_bitcast_fusion.1
  123.2 1.3 convolution_bitcast_fusion.3
  124.5 1.3 convolution_bitcast_fusion
  125.8 1.3 convolution_bitcast_fusion.2
  127.1 1.3 convolution_bitcast_fusion.7
  128.4 1.3 convolution_bitcast_fusion.6
  130.0 0.6 collective-permute-start.22
  130.8 1.3 convolution_bitcast_fusion.5
  132.1 1.3 convolution_bitcast_fusion.4
  133.5 0.6 collective-permute-start.20
  134.1 0.2 fusion.8
  134.5 3.0 %collective-permute-start.23 = (bf16[2,256,512]{2,1,0:T(8,128)(2,1)S(1)}, bf16[2,256,512]{2,1,0:T(8,128)(2,1)S(1)}, u32[]{:S(2)}, u32[]{:S(2)}) collective-permute-start(bf16[2,256,512]{2,1,0:T(8,128)(2,1)S(1)} %pad_maximum_fusion.3), channel_id=1, source_target_pairs={{0,48},{1,49},{2,50},{3,51},{4,52},{5,53},{6,54},{7,55},{8,56},{9,... | collective-permute-start | bytes 1572872 | tf_op jit(solution)/shard_map/ppermute | solution.py:30
  137.5 0.2 fusion.14
  137.9 1.3 collective-permute-start.19
  139.2 0.2 fusion.11
  139.6 0.7 collective-permute-start.21
  140.3 19.9 %collective-permute-done.23 = bf16[2,256,512]{2,1,0:T(8,128)(2,1)S(1)} collective-permute-done((bf16[2,256,512]{2,1,0:T(8,128)(2,1)S(1)}, bf16[2,256,512]{2,1,0:T(8,128)(2,1)S(1)}, u32[]{:S(2)}, u32[]{:S(2)}) %collective-permute-start.23) | collective-permute-done | bytes 524320 | tf_op jit(solution)/shard_map/ppermute | solution.py:30
  160.2 4.2 %collective-permute-done.21 = bf16[2,256,512]{2,1,0:T(8,128)(2,1)S(1)} collective-permute-done((bf16[2,256,512]{2,1,0:T(8,128)(2,1)S(1)}, bf16[2,256,512]{2,1,0:T(8,128)(2,1)S(1)}, u32[]{:S(2)}, u32[]{:S(2)}) %collective-permute-start.21) | collective-permute-done | bytes 524320 | tf_op jit(solution)/shard_map/ppermute | solution.py:30
  164.4 0.4 fusion.5
  164.9 2.4 %collective-permute-start.25 = (f32[256,512]{1,0:T(8,128)S(1)}, f32[256,512]{1,0:T(8,128)S(1)}, u32[]{:S(2)}, u32[]{:S(2)}) collective-permute-start(f32[256,512]{1,0:T(8,128)S(1)} %fusion.25), channel_id=1, source_target_pairs={{0,0},{1,16},{2,2},{3,18},{4,4},{5,20},{6,6},{7,22},{8,1},{9,17},{... | collective-permute-start | bytes 1572872 | tf_op jit(solution)/shard_map/ppermute | solution.py:30
  167.3 15.6 %collective-permute-done.25 = f32[256,512]{1,0:T(8,128)S(1)} collective-permute-done((f32[256,512]{1,0:T(8,128)S(1)}, f32[256,512]{1,0:T(8,128)S(1)}, u32[]{:S(2)}, u32[]{:S(2)}) %collective-permute-start.25) | collective-permute-done | bytes 524320 | tf_op jit(solution)/shard_map/ppermute | solution.py:30
  182.9 0.8 copy.26
  (65 shorter events, 3.4 us)
Async XLA Ops:
  0.0 30.8 %copy-start = (f32[1024,512]{1,0:T(8,128)S(1)}, f32[1024,512]{1,0:T(8,128)}, u32[]{:S(2)}) copy-start(f32[1024,512]{1,0:T(8,128)} %param.2) | copy-start | bytes 6291460
  1.1 8.5 %collective-permute-start = (f32[32,512]{1,0:T(8,128)S(1)}, f32[32,512]{1,0:T(8,128)S(1)}, u32[]{:S(2)}, u32[]{:S(2)}) collective-permute-start(f32[32,512]{1,0:T(8,128)S(1)} %maximum_maximum_fusion.2.value), channel_id=1, source_target_pairs={{0,1},{1,0},{2,3},{3,2},{4,5},{5,4},{6,7},{7,6},{8,9},{9,8},{10,11... | collective-permute-start | bytes 196616 | tf_op jit(solution)/shard_map/ppermute | solution.py:30
  7.8 9.6 %collective-permute-start.4 = (f32[32,1024]{1,0:T(8,128)S(1)}, f32[32,1024]{1,0:T(8,128)S(1)}, u32[]{:S(2)}, u32[]{:S(2)}) collective-permute-start(f32[32,1024]{1,0:T(8,128)S(1)} %fusion.1), channel_id=1, source_target_pairs={{0,1},{1,0},{2,3},{3,2},{4,5},{5,4},{6,7},{7,6},{8,9},{9,8},{10,11... | collective-permute-start | bytes 393224 | tf_op jit(solution)/shard_map/ppermute | solution.py:30
  11.4 9.3 %collective-permute-start.3 = (f32[2,32,512]{2,1,0:T(8,128)S(1)}, f32[2,32,512]{2,1,0:T(8,128)S(1)}, u32[]{:S(2)}, u32[]{:S(2)}) collective-permute-start(f32[2,32,512]{2,1,0:T(8,128)S(1)} %pad_maximum_fusion.4), channel_id=1, source_target_pairs={{0,2},{1,3},{2,4},{3,5},{4,6},{5,7},{6,0},{7,1},{8,10},{9,11},{10,... | collective-permute-start | bytes 393224 | tf_op jit(solution)/shard_map/ppermute | solution.py:30
  13.0 9.6 %collective-permute-start.2 = (f32[2,32,512]{2,1,0:T(8,128)S(1)}, f32[2,32,512]{2,1,0:T(8,128)S(1)}, u32[]{:S(2)}, u32[]{:S(2)}) collective-permute-start(f32[2,32,512]{2,1,0:T(8,128)S(1)} %pad_maximum_fusion.4), channel_id=1, source_target_pairs={{0,4},{1,5},{2,6},{3,7},{4,0},{5,1},{6,2},{7,3},{8,12},{9,13},{10,... | collective-permute-start | bytes 393224 | tf_op jit(solution)/shard_map/ppermute | solution.py:30
  15.7 7.3 %collective-permute-start.1 = (f32[2,32,512]{2,1,0:T(8,128)S(1)}, f32[2,32,512]{2,1,0:T(8,128)S(1)}, u32[]{:S(2)}, u32[]{:S(2)}) collective-permute-start(f32[2,32,512]{2,1,0:T(8,128)S(1)} %pad_maximum_fusion.4), channel_id=1, source_target_pairs={{0,6},{1,7},{2,0},{3,1},{4,2},{5,3},{6,4},{7,5},{8,14},{9,15},{10,... | collective-permute-start | bytes 393224 | tf_op jit(solution)/shard_map/ppermute | solution.py:30
  17.4 11.3 %collective-permute-start.7 = (f32[32,1024]{1,0:T(8,128)S(1)}, f32[32,1024]{1,0:T(8,128)S(1)}, u32[]{:S(2)}, u32[]{:S(2)}) collective-permute-start(f32[32,1024]{1,0:T(8,128)S(1)} %add.201), channel_id=1, source_target_pairs={{0,2},{1,3},{2,4},{3,5},{4,6},{5,7},{6,0},{7,1},{8,10},{9,11},{10,... | collective-permute-start | bytes 393224 | tf_op jit(solution)/shard_map/ppermute | solution.py:30
  18.0 10.7 %collective-permute-start.6 = (f32[32,1024]{1,0:T(8,128)S(1)}, f32[32,1024]{1,0:T(8,128)S(1)}, u32[]{:S(2)}, u32[]{:S(2)}) collective-permute-start(f32[32,1024]{1,0:T(8,128)S(1)} %add.201), channel_id=1, source_target_pairs={{0,6},{1,7},{2,0},{3,1},{4,2},{5,3},{6,4},{7,5},{8,14},{9,15},{10,... | collective-permute-start | bytes 393224 | tf_op jit(solution)/shard_map/ppermute | solution.py:30
  20.7 8.1 %collective-permute-start.5 = (f32[32,1024]{1,0:T(8,128)S(1)}, f32[32,1024]{1,0:T(8,128)}, u32[]{:S(2)}, u32[]{:S(2)}) collective-permute-start(f32[32,1024]{1,0:T(8,128)S(1)} %add.201), channel_id=1, source_target_pairs={{0,4},{1,5},{2,6},{3,7},{4,0},{5,1},{6,2},{7,3},{8,12},{9,13},{10,... | collective-permute-start | bytes 393224 | tf_op jit(solution)/shard_map/ppermute | solution.py:30
  29.9 5.0 %collective-permute-start.8 = (f32[32,1024]{1,0:T(8,128)S(1)}, f32[32,1024]{1,0:T(8,128)S(1)}, u32[]{:S(2)}, u32[]{:S(2)}) collective-permute-start(f32[32,1024]{1,0:T(8,128)S(1)} %fusion.29.value), channel_id=1, source_target_pairs={{0,65},{1,64},{2,67},{3,66},{4,69},{5,68},{6,71},{7,70},{8,73},{9,... | collective-permute-start | bytes 393224 | tf_op jit(solution)/shard_map/ppermute | solution.py:30
  35.0 21.1 %collective-permute-start.13 = (bf16[1024,512]{1,0:T(8,128)(2,1)}, bf16[1024,512]{1,0:T(8,128)(2,1)S(1)}, u32[]{:S(2)}, u32[]{:S(2)}) collective-permute-start(bf16[1024,512]{1,0:T(8,128)(2,1)} %fusion), channel_id=1, source_target_pairs={{0,64},{1,65},{2,66},{3,67},{4,68},{5,69},{6,70},{7,71},{8,72},{9,... | collective-permute-start | bytes 3145736 | tf_op jit(solution)/shard_map/ppermute | solution.py:30
  36.9 21.7 %collective-permute-start.12 = (bf16[1024,512]{1,0:T(8,128)(2,1)}, bf16[1024,512]{1,0:T(8,128)(2,1)S(1)}, u32[]{:S(2)}, u32[]{:S(2)}) collective-permute-start(bf16[1024,512]{1,0:T(8,128)(2,1)} %fusion), channel_id=1, source_target_pairs={{0,65},{1,64},{2,67},{3,66},{4,69},{5,68},{6,71},{7,70},{8,73},{9,... | collective-permute-start | bytes 3145736 | tf_op jit(solution)/shard_map/ppermute | solution.py:30
  38.2 26.1 %collective-permute-start.11 = (bf16[1024,256]{1,0:T(8,128)(2,1)S(1)}, bf16[1024,256]{1,0:T(8,128)(2,1)S(1)}, u32[]{:S(2)}, u32[]{:S(2)}) collective-permute-start(bf16[1024,256]{1,0:T(8,128)(2,1)S(1)} %constant_dynamic-slice_fusion.1), channel_id=1, source_target_pairs={{0,2},{1,3},{2,4},{3,5},{4,6},{5,7},{6,0},{7,1},{8,10},{9,11},{10,... | collective-permute-start | bytes 1572872 | tf_op jit(solution)/shard_map/ppermute | solution.py:30
  38.7 46.7 %collective-permute-start.10 = (bf16[1024,256]{1,0:T(8,128)(2,1)S(1)}, bf16[1024,256]{1,0:T(8,128)(2,1)S(1)}, u32[]{:S(2)}, u32[]{:S(2)}) collective-permute-start(bf16[1024,256]{1,0:T(8,128)(2,1)S(1)} %constant_dynamic-slice_fusion.1), channel_id=1, source_target_pairs={{0,4},{1,5},{2,6},{3,7},{4,0},{5,1},{6,2},{7,3},{8,12},{9,13},{10,... | collective-permute-start | bytes 1572872 | tf_op jit(solution)/shard_map/ppermute | solution.py:30
  41.9 47.8 %collective-permute-start.9 = (bf16[1024,256]{1,0:T(8,128)(2,1)S(1)}, bf16[1024,256]{1,0:T(8,128)(2,1)S(1)}, u32[]{:S(2)}, u32[]{:S(2)}) collective-permute-start(bf16[1024,256]{1,0:T(8,128)(2,1)S(1)} %constant_dynamic-slice_fusion.1), channel_id=1, source_target_pairs={{0,6},{1,7},{2,0},{3,1},{4,2},{5,3},{6,4},{7,5},{8,14},{9,15},{10,... | collective-permute-start | bytes 1572872 | tf_op jit(solution)/shard_map/ppermute | solution.py:30
  59.7 30.0 %collective-permute-start.16 = (bf16[1024,256]{1,0:T(8,128)(2,1)S(1)}, bf16[1024,256]{1,0:T(8,128)(2,1)S(1)}, u32[]{:S(2)}, u32[]{:S(2)}) collective-permute-start(bf16[1024,256]{1,0:T(8,128)(2,1)S(1)} %constant_dynamic-slice_fusion), channel_id=1, source_target_pairs={{0,2},{1,3},{2,4},{3,5},{4,6},{5,7},{6,0},{7,1},{8,10},{9,11},{10,... | collective-permute-start | bytes 1572872 | tf_op jit(solution)/shard_map/ppermute | solution.py:30
  61.2 28.6 %collective-permute-start.15 = (bf16[1024,256]{1,0:T(8,128)(2,1)S(1)}, bf16[1024,256]{1,0:T(8,128)(2,1)S(1)}, u32[]{:S(2)}, u32[]{:S(2)}) collective-permute-start(bf16[1024,256]{1,0:T(8,128)(2,1)S(1)} %constant_dynamic-slice_fusion), channel_id=1, source_target_pairs={{0,4},{1,5},{2,6},{3,7},{4,0},{5,1},{6,2},{7,3},{8,12},{9,13},{10,... | collective-permute-start | bytes 1572872 | tf_op jit(solution)/shard_map/ppermute | solution.py:30
  64.4 25.4 %collective-permute-start.14 = (bf16[1024,256]{1,0:T(8,128)(2,1)S(1)}, bf16[1024,256]{1,0:T(8,128)(2,1)S(1)}, u32[]{:S(2)}, u32[]{:S(2)}) collective-permute-start(bf16[1024,256]{1,0:T(8,128)(2,1)S(1)} %constant_dynamic-slice_fusion), channel_id=1, source_target_pairs={{0,6},{1,7},{2,0},{3,1},{4,2},{5,3},{6,4},{7,5},{8,14},{9,15},{10,... | collective-permute-start | bytes 1572872 | tf_op jit(solution)/shard_map/ppermute | solution.py:30
  85.4 29.4 %collective-permute-start.17 = (bf16[1024,512]{1,0:T(8,128)(2,1)}, bf16[1024,512]{1,0:T(8,128)(2,1)S(1)}, u32[]{:S(2)}, u32[]{:S(2)}) collective-permute-start(bf16[1024,512]{1,0:T(8,128)(2,1)} %fusion), channel_id=1, source_target_pairs={{0,1},{1,0},{2,3},{3,2},{4,5},{5,4},{6,7},{7,6},{8,9},{9,8},{10,11... | collective-permute-start | bytes 3145736 | tf_op jit(solution)/shard_map/ppermute | solution.py:30
  129.8 10.5 %collective-permute-start.24 = (f32[2,256,512]{2,1,0:T(8,128)S(1)}, f32[2,256,512]{2,1,0:T(8,128)S(1)}, u32[]{:S(2)}, u32[]{:S(2)}) collective-permute-start(f32[2,256,512]{2,1,0:T(8,128)S(1)} %fusion.2), channel_id=1, source_target_pairs={{0,8},{1,9},{2,10},{3,11},{4,12},{5,13},{6,14},{7,15},{8,0},{9,1},... | collective-permute-start | bytes 3145736 | tf_op jit(solution)/shard_map/ppermute | solution.py:30
  130.0 4.0 %collective-permute-start.22 = (f32[2,256,512]{2,1,0:T(8,128)S(1)}, f32[2,256,512]{2,1,0:T(8,128)S(1)}, u32[]{:S(2)}, u32[]{:S(2)}) collective-permute-start(f32[2,256,512]{2,1,0:T(8,128)S(1)} %fusion.6), channel_id=1, source_target_pairs={{0,8},{1,9},{2,10},{3,11},{4,12},{5,13},{6,14},{7,15},{8,0},{9,1},... | collective-permute-start | bytes 3145736 | tf_op jit(solution)/shard_map/ppermute | solution.py:30
  130.7 6.8 %collective-permute-start.18 = (f32[2,256,512]{2,1,0:T(8,128)S(1)}, f32[2,256,512]{2,1,0:T(8,128)S(1)}, u32[]{:S(2)}, u32[]{:S(2)}) collective-permute-start(f32[2,256,512]{2,1,0:T(8,128)S(1)} %fusion.12), channel_id=1, source_target_pairs={{0,8},{1,9},{2,10},{3,11},{4,12},{5,13},{6,14},{7,15},{8,0},{9,1},... | collective-permute-start | bytes 3145736 | tf_op jit(solution)/shard_map/ppermute | solution.py:30
  133.5 5.7 %collective-permute-start.20 = (f32[2,256,512]{2,1,0:T(8,128)S(1)}, f32[2,256,512]{2,1,0:T(8,128)S(1)}, u32[]{:S(2)}, u32[]{:S(2)}) collective-permute-start(f32[2,256,512]{2,1,0:T(8,128)S(1)} %fusion.9), channel_id=1, source_target_pairs={{0,8},{1,9},{2,10},{3,11},{4,12},{5,13},{6,14},{7,15},{8,0},{9,1},... | collective-permute-start | bytes 3145736 | tf_op jit(solution)/shard_map/ppermute | solution.py:30
  134.5 25.8 %collective-permute-start.23 = (bf16[2,256,512]{2,1,0:T(8,128)(2,1)S(1)}, bf16[2,256,512]{2,1,0:T(8,128)(2,1)S(1)}, u32[]{:S(2)}, u32[]{:S(2)}) collective-permute-start(bf16[2,256,512]{2,1,0:T(8,128)(2,1)S(1)} %pad_maximum_fusion.3), channel_id=1, source_target_pairs={{0,48},{1,49},{2,50},{3,51},{4,52},{5,53},{6,54},{7,55},{8,56},{9,... | collective-permute-start | bytes 1572872 | tf_op jit(solution)/shard_map/ppermute | solution.py:30
  137.9 22.3 %collective-permute-start.19 = (bf16[2,256,512]{2,1,0:T(8,128)(2,1)S(1)}, bf16[2,256,512]{2,1,0:T(8,128)(2,1)S(1)}, u32[]{:S(2)}, u32[]{:S(2)}) collective-permute-start(bf16[2,256,512]{2,1,0:T(8,128)(2,1)S(1)} %pad_maximum_fusion.1), channel_id=1, source_target_pairs={{0,32},{1,33},{2,34},{3,35},{4,36},{5,37},{6,38},{7,39},{8,40},{9,... | collective-permute-start | bytes 1572872 | tf_op jit(solution)/shard_map/ppermute | solution.py:30
  139.6 24.8 %collective-permute-start.21 = (bf16[2,256,512]{2,1,0:T(8,128)(2,1)S(1)}, bf16[2,256,512]{2,1,0:T(8,128)(2,1)S(1)}, u32[]{:S(2)}, u32[]{:S(2)}) collective-permute-start(bf16[2,256,512]{2,1,0:T(8,128)(2,1)S(1)} %pad_maximum_fusion.2), channel_id=1, source_target_pairs={{0,16},{1,17},{2,18},{3,19},{4,20},{5,21},{6,22},{7,23},{8,24},{9,... | collective-permute-start | bytes 1572872 | tf_op jit(solution)/shard_map/ppermute | solution.py:30
  164.9 18.0 %collective-permute-start.25 = (f32[256,512]{1,0:T(8,128)S(1)}, f32[256,512]{1,0:T(8,128)S(1)}, u32[]{:S(2)}, u32[]{:S(2)}) collective-permute-start(f32[256,512]{1,0:T(8,128)S(1)} %fusion.25), channel_id=1, source_target_pairs={{0,0},{1,16},{2,2},{3,18},{4,4},{5,20},{6,6},{7,22},{8,1},{9,17},{... | collective-permute-start | bytes 1572872 | tf_op jit(solution)/shard_map/ppermute | solution.py:30
where the time goes:
time: 184 us
  waiting for transfers between devices  57.3 us (31%)
  other arithmetic  41 us (22%)
  starting transfers between devices  39.8 us (22%)
  Pallas kernels  23.2 us (13%)
  matrix products  19.8 us (11%)
  local copies, waits for them, and re-layouts  2.14 us (1%)
    ppermute x26, waiting for transfers between devices, move(): return lax.ppermute(value, AXES, pairs(where))  57.3 us
    ppermute x26, starting transfers between devices, move(): return lax.ppermute(value, AXES, pairs(where))  39.8 us
    concatenate x1, other arithmetic, body(): jnp.concatenate([jnp.concatenate(near_rows, axis=1), jnp.concatenate(far_...  23.5 us
    pallas_call x1, Pallas kernels, spreads(): pl.pallas_call(spread_kernel, grid=(rows // TILE,), in_specs=[pl.BlockSpe...  19.9 us
    dot_general x8, matrix products, gram(): lax.dot_general(a, b, (((0,), (0,)), ((), ())), preferred_element_type=jn...  10.4 us
    select_n x2, other arithmetic, in_order(): jnp.where(zh == 0, a, b)  3.82 us
  transfers between devices with their start and end apart: 26, of which 7 were waited for; matrix products, arithmetic and copies ran while one was open for 25% of the time, Pallas kernels for 12%

commit v1 on v0

--- a/solution.py
+++ b/solution.py
@@ -91,16 +91,19 @@
     return jnp.clip(0.5 * fitted, 0.02, 0.98)
 
 
-def spread_kernel(left, right, out):
-    @pl.loop(0, right.shape[1] // TILE)
-    def _(k):
-        at = pl.ds(pl.multiple_of(k * TILE, TILE), TILE)
-        freq = frequencies(left[...], right[:, at])
-        out[:, at] = jnp.sqrt(freq * (1.0 - freq)).astype(jnp.bfloat16)
+def spread_kernel(left, right, *outs):
+    flat = left[...].T
+    each = outs[0].shape[1]
+    for n, out in enumerate(outs):
+        for k in range(0, each, TILE):
+            fitted = jnp.dot(flat, right[:, n * each + k : n * each + k + TILE], preferred_element_type=jnp.float32)
+            freq = jnp.clip(0.5 * fitted, 0.02, 0.98)
+            square = freq * (1.0 - freq)
+            out[:, k : k + TILE] = (square * lax.rsqrt(square)).astype(jnp.bfloat16)
 
 
 def spreads(left, right):
-    rows, columns = left.shape[1], right.shape[1]
+    rows, columns = left.shape[1], right.shape[1] // 2
     return pl.pallas_call(
         spread_kernel,
         grid=(rows // TILE,),
@@ -108,31 +111,59 @@
             pl.BlockSpec((left.shape[0], TILE), lambda i: (0, i)),
             pl.BlockSpec(right.shape, lambda i: (0, 0)),
         ],
-        out_specs=pl.BlockSpec((TILE, columns), lambda i: (i, 0)),
-        out_shape=jax.ShapeDtypeStruct((rows, columns), jnp.bfloat16),
+        out_specs=[pl.BlockSpec((TILE, columns), lambda i: (i, 0))] * 2,
+        out_shape=[jax.ShapeDtypeStruct((rows, columns), jnp.bfloat16)] * 2,
         compiler_params=pltpu.CompilerParams(vmem_limit_bytes=12 << 20),
         name="spreads",
     )(left, right)
 
 
-def open_kernel(code, raw, resid, spread):
-    seen = code[...] < 3.0
-    resid[...] = jnp.where(seen, code[...], jnp.zeros_like(code))
-    spread[...] = jnp.where(seen, raw[...], jnp.zeros_like(code))
-
-
-def open_code(code, raw, which):
-    rows, columns = code.shape
-    block = pl.BlockSpec((TILE, columns), lambda i: (i, 0))
+def open_piece(code, raw, resid, spread):
+    @pl.loop(0, code.shape[0] // TILE)
+    def _(k):
+        at = pl.ds(pl.multiple_of(k * TILE, TILE), TILE)
+        value = code[at, :]
+        seen = value < 3.0
+        zero = jnp.zeros_like(value)
+        resid[at, :] = jnp.where(seen, value, zero)
+        spread[at, :] = jnp.where(seen, raw[at, :], zero)
+
+
+def open_rows_kernel(*refs):
+    raw, resid, spread = refs[8:]
+    for k in range(8):
+        length, width = refs[k].shape
+        at = pl.ds(k // 4 * length, length)
+        open_piece(
+            refs[k],
+            raw.at[at, pl.ds(k % 4 * width, width)],
+            resid.at[k % 4, at],
+            spread.at[k % 4, at],
+        )
+
+
+def open_columns_kernel(zh, *refs):
+    raw, resid, spread = refs[4:]
+    for k in range(4):
+        length, width = refs[k].shape
+        first = zh[0] if k % 2 == 0 else 1 - zh[0]
+        at = (pl.ds(k // 2 * length, length), pl.ds(pl.multiple_of(first * width, width), width))
+        open_piece(refs[k], raw.at[at], resid.at[at], spread.at[at])
+
+
+VMEM = pl.BlockSpec(memory_space=pltpu.VMEM)
+SMEM = pl.BlockSpec(memory_space=pltpu.SMEM)
+
+
+def open_code(kernel, shape, scalars, arrays):
     return pl.pallas_call(
-        open_kernel,
-        grid=(rows // TILE,),
-        in_specs=[block, pl.BlockSpec((TILE, columns), lambda i: (i, which))],
-        out_specs=[block, block],
-        out_shape=[jax.ShapeDtypeStruct(code.shape, jnp.bfloat16)] * 2,
+        kernel,
+        in_specs=[SMEM] * len(scalars) + [VMEM] * len(arrays),
+        out_specs=[VMEM] * 2,
+        out_shape=[jax.ShapeDtypeStruct(shape, jnp.bfloat16)] * 2,
         compiler_params=pltpu.CompilerParams(vmem_limit_bytes=8 << 20),
-        name="open_code",
-    )(code, raw)
+        name=kernel.__name__,
+    )(*scalars, *arrays)
 
 
 def gram(a, b):
@@ -178,22 +209,30 @@
     up, down = from_z(code, 1), from_z(code, 3)
     near_half = my_half(code)
     near_rows = [near_half] + [from_x(near_half, d) for d in (1, 2, 3)]
-    raw = spreads(jnp.concatenate([near6, terms(coef_far, LEFT)], axis=1), all6)
+    raw_columns, raw_rows = spreads(jnp.concatenate([near6, terms(coef_far, LEFT)], axis=1), all6)
+    up, down, raw_columns, raw_rows = lax.optimization_barrier((up, down, raw_columns, raw_rows))
     far_same = jnp.where(zl == 0, up, down)
     far_other = jnp.where(zl == 0, down, up)
     far_half = my_half(far_same)
     far_rows = [far_half] + [from_x(far_half, d) for d in (1, 2, 3)]
     across = from_z(lax.optimization_barrier((code, up, down))[0], 2)
-    rows = jnp.concatenate([jnp.concatenate(near_rows, axis=1), jnp.concatenate(far_rows, axis=1)], axis=0)
-    row_resid, row_spread = open_code(rows, raw, 1)
-    columns = jnp.concatenate([in_order(code, across), in_order(far_same, far_other)], axis=0)
-    col_resid, col_spread = open_code(columns, raw, 0)
-
+    count = 2 * code.shape[0]
+    row_resid, row_spread = open_code(
+        open_rows_kernel, (4, count, half), [], near_rows + far_rows + [raw_rows]
+    )
+    col_resid, col_spread = open_code(
+        open_columns_kernel,
+        (count, 2 * here),
+        [jnp.reshape(zh, (1,)).astype(jnp.int32)],
+        [code, across, far_same, far_other, raw_columns],
+    )
     sums = None
     for step in (2, 1, 3, 0):
-        at = (0, (rows_at((y + step) % 4, zh) - x) % 4 * half)
-        numer = gram(lax.dynamic_slice(row_resid, at, (rows.shape[0], half)), col_resid)
-        denom = gram(lax.dynamic_slice(row_spread, at, (rows.shape[0], half)), col_spread)
+        d = (rows_at((y + step) % 4, zh) - x) % 4
+        if sums is not None:
+            d, _ = lax.optimization_barrier((d, give))
+        numer = gram(lax.dynamic_index_in_dim(row_resid, d, 0, False), col_resid)
+        denom = gram(lax.dynamic_index_in_dim(row_spread, d, 0, False), col_spread)
         both = jnp.stack([numer, denom])
         keep = lax.dynamic_slice(both, (0, 0, c * here), (2, half, here))
         give = lax.dynamic_slice(both, (0, 0, (1 - c) * here), (2, half, here))

time: 184 us -> 181 us (0.984)
  other arithmetic: 41 us -> 18.2 us
  matrix products: 19.8 us -> 31.6 us
  Pallas kernels: 23.2 us -> 12.5 us
  starting transfers between devices: 39.8 us -> 48.6 us
  local copies, waits for them, and re-layouts: 2.14 us -> 9.68 us
    concatenate x3 -> x1, other arithmetic: 26.3 us -> 0.06 us  [body(): jnp.concatenate([near6, terms(coef_far, LEFT)], axis=1)]
    pallas_call x1, Pallas kernels: 19.9 us -> 6.13 us  [spreads(): pl.pallas_call(spread_kernel, grid=(rows // TILE,), in_specs=[pl.BlockSpe...]
    dot_general x8, matrix products: 10.4 us -> 22.4 us  [gram(): lax.dot_general(a, b, (((0,), (0,)), ((), ())), preferred_element_type=jn...]
    ppermute x26, starting transfers between devices: 39.8 us -> 48.6 us  [move(): return lax.ppermute(value, AXES, pairs(where))]
    unnamed x6 -> x42, local copies, waits for them, and re-layouts: 0.82 us -> 7.77 us
    add x3, other arithmetic: 0.63 us -> 4.44 us  [body(): merged = keep + flip(give)]
    select_n x3 -> x1, other arithmetic: 5.04 us -> 1.68 us  [body(): far_other = jnp.where(zl == 0, down, up)]
    another operation x4, other arithmetic: 0.38 us -> 3.54 us  [body(): both = jnp.stack([numer, denom])]
  transfers between devices with their start and end apart: 26 -> 26, of which waited for: 7 -> 12; matrix products, arithmetic and copies ran while one was open for 25% -> 26% of each run, Pallas kernels for 12% -> 5%
where the time goes in v1:
time: 181 us; the launch traced here: 179 us
  waiting for transfers between devices  58.1 us (32%)
  starting transfers between devices  48.6 us (27%)
  matrix products  31.6 us (17%)
  other arithmetic  18.2 us (10%)
  Pallas kernels  12.5 us (7%)
  local copies, waits for them, and re-layouts  9.68 us (5%)
    ppermute x26, waiting for transfers between devices, move(): return lax.ppermute(value, AXES, pairs(where))  58.1 us
    ppermute x26, starting transfers between devices, move(): return lax.ppermute(value, AXES, pairs(where))  48.6 us
    dot_general x8, matrix products, gram(): lax.dot_general(a, b, (((0,), (0,)), ((), ())), preferred_element_type=jn...  22.4 us
    unnamed x42, local copies, waits for them, and re-layouts  7.77 us
    pallas_call x2, Pallas kernels, open_code(): pl.pallas_call(kernel, in_specs=[SMEM] * len(scalars) + [VMEM] * len(arra...  6.17 us
    pallas_call x1, Pallas kernels, spreads(): pl.pallas_call(spread_kernel, grid=(rows // TILE,), in_specs=[pl.BlockSpe...  6.13 us
    add x3, other arithmetic, body(): merged = keep + flip(give)  4.44 us
  transfers between devices with their start and end apart: 26, of which 12 were waited for; matrix products, arithmetic and copies ran while one was open for 26% of the time, Pallas kernels for 5%

profile of v1, /device:TPU:32, one launch (start us, length us, event | category | flops | bytes accessed | tf_op | source)
XLA Modules:
  0.0 179.1 jit_solution(11135891814707164370)
XLA Ops:
  0.1 0.9 maximum_maximum_fusion.value
  1.0 3.1 %collective-permute-start = (f32[32,512]{1,0:T(8,128)S(1)}, f32[32,512]{1,0:T(8,128)S(1)}, u32[]{:S(2)}, u32[]{:S(2)}) collective-permute-start(f32[32,512]{1,0:T(8,128)S(1)} %maximum_maximum_fusion.value), channel_id=1, source_target_pairs={{0,1},{1,0},{2,3},{3,2},{4,5},{5,4},{6,7},{7,6},{8,9},{9,8},{10,11... | collective-permute-start | bytes 196616 | tf_op jit(solution)/shard_map/ppermute | solution.py:30
  4.0 3.6 %fusion.1 = f32[32,1024]{1,0:T(8,128)S(1)} fusion(f32[1024,512]{1,0:T(8,128)} %param.2, f32[20,512]{1,0:T(8,128)} %param.3, f32[32]{0:T(128)S(1)} %pad.25.clone, f32[32]{0:T(128)S(1)} %pad.23.clone), kind=kOutput, calls=%fused_computation.19 | convolution fusion | flops 202407936 | bytes 2269440 | tf_op jit(solution)/shard_map/dot_general | solution.py:183
  7.6 0.6 collective-permute-start.4
  8.3 1.1 fusion.71
  9.5 0.9 select_dynamic-update-slice_fusion.1
  10.4 0.9 select_dynamic-update-slice_fusion
  11.3 1.6 collective-permute-start.3
  12.8 2.7 %collective-permute-start.2 = (f32[2,32,512]{2,1,0:T(8,128)S(1)}, f32[2,32,512]{2,1,0:T(8,128)S(1)}, u32[]{:S(2)}, u32[]{:S(2)}) collective-permute-start(f32[2,32,512]{2,1,0:T(8,128)S(1)} %pad_maximum_fusion.4), channel_id=1, source_target_pairs={{0,4},{1,5},{2,6},{3,7},{4,0},{5,1},{6,2},{7,3},{8,12},{9,13},{10,... | collective-permute-start | bytes 393224 | tf_op jit(solution)/shard_map/ppermute | solution.py:30
  15.6 1.4 collective-permute-start.1
  17.2 0.6 collective-permute-start.5
  17.8 2.8 %collective-permute-start.6 = (f32[32,1024]{1,0:T(8,128)S(1)}, f32[32,1024]{1,0:T(8,128)S(1)}, u32[]{:S(2)}, u32[]{:S(2)}) collective-permute-start(f32[32,1024]{1,0:T(8,128)S(1)} %add.202), channel_id=1, source_target_pairs={{0,6},{1,7},{2,0},{3,1},{4,2},{5,3},{6,4},{7,5},{8,14},{9,15},{10,... | collective-permute-start | bytes 393224 | tf_op jit(solution)/shard_map/ppermute | solution.py:30
  21.0 1.2 collective-permute-done.2
  22.6 0.6 collective-permute-done.1
  23.7 1.9 %cholesky.17 = f32[21,21]{1,0:T(8,128)S(1)} custom-call(f32[21,21]{1,0:T(8,128)S(1)} %fusion.56), custom_call_target="Cholesky" | custom-call | tf_op jit(solution)/shard_map/jit(cholesky)/cholesky | solution.py:191
  25.7 0.6 compare_reduce_fusion
  26.3 0.6 fusion.51
  27.0 1.6 custom-call.10
  29.8 2.4 %fusion.refs_0_ = bf16[1024,512]{1,0:T(8,128)(2,1)S(1)} fusion(f32[1024,512]{1,0:T(8,128)} %param.2, bf16[192,1024]{1,0:T(8,128)(2,1)S(1)} %terms.4, bf16[192,512]{1,0:T(8,128)(2,1)S(1)} %terms.5), kind=kOutput, calls=%fused_computation.18 | convolution fusion | flops 205520896 | bytes 3735552 | tf_op jit(solution)/shard_map/dot_general | solution.py:90
  32.2 3.5 %collective-permute-done.8.value = f32[32,1024]{1,0:T(8,128)S(1)} collective-permute-done((f32[32,1024]{1,0:T(8,128)S(1)}, f32[32,1024]{1,0:T(8,128)S(1)}, u32[]{:S(2)}, u32[]{:S(2)}) %collective-permute-start.8) | collective-permute-done | bytes 131104 | tf_op jit(solution)/shard_map/ppermute | solution.py:30
  35.7 1.2 collective-permute-start.12
  37.0 0.8 collective-permute-start.13
  37.9 0.8 constant_dynamic-slice_fusion.1.refs_0_
  38.8 2.5 %collective-permute-start.10 = (bf16[1024,256]{1,0:T(8,128)(2,1)}, bf16[1024,256]{1,0:T(8,128)(2,1)}, u32[]{:S(2)}, u32[]{:S(2)}) collective-permute-start(bf16[1024,256]{1,0:T(8,128)(2,1)} %constant_dynamic-slice_fusion.1.refs_0_), channel_id=1, source_target_pairs={{0,4},{1,5},{2,6},{3,7},{4,0},{5,1},{6,2},{7,3},{8,12},{9,13},{10,... | collective-permute-start | bytes 1572872 | tf_op jit(solution)/shard_map/ppermute | solution.py:30
  41.2 2.6 %collective-permute-start.11 = (bf16[1024,256]{1,0:T(8,128)(2,1)}, bf16[1024,256]{1,0:T(8,128)(2,1)}, u32[]{:S(2)}, u32[]{:S(2)}) collective-permute-start(bf16[1024,256]{1,0:T(8,128)(2,1)} %constant_dynamic-slice_fusion.1.refs_0_), channel_id=1, source_target_pairs={{0,2},{1,3},{2,4},{3,5},{4,6},{5,7},{6,0},{7,1},{8,10},{9,11},{10,... | collective-permute-start | bytes 1572872 | tf_op jit(solution)/shard_map/ppermute | solution.py:30
  43.9 6.1 %spreads.1 = (bf16[2048,1024]{1,0:T(8,128)(2,1)S(1)}, bf16[2048,1024]{1,0:T(8,128)(2,1)S(1)}) custom-call(bf16[192,2048]{1,0:T(8,128)(2,1)S(1)} %pad_maximum_fusion.left, bf16[192,2048]{1,0:T(8,128)(2,1)S(1)} %terms.7.right), custom_call_target="tpu_custom_call" | custom-call | tf_op jit(solution)/shard_map/spreads/pallas_call | solution.py:107
  50.1 2.0 %copy-done = bf16[2048,1024]{1,0:T(8,128)(2,1)} copy-done((bf16[2048,1024]{1,0:T(8,128)(2,1)}, bf16[2048,1024]{1,0:T(8,128)(2,1)S(1)}, u32[]{:S(2)}) %copy-start) | copy-done | bytes 4194328
  52.0 2.0 %copy-done.2 = bf16[2048,1024]{1,0:T(8,128)(2,1)} copy-done((bf16[2048,1024]{1,0:T(8,128)(2,1)}, bf16[2048,1024]{1,0:T(8,128)(2,1)S(1)}, u32[]{:S(2)}) %copy-start.2) | copy-done | bytes 4194328
  54.1 2.2 %collective-permute-done.12 = bf16[1024,512]{1,0:T(8,128)(2,1)} collective-permute-done((bf16[1024,512]{1,0:T(8,128)(2,1)S(1)}, bf16[1024,512]{1,0:T(8,128)(2,1)}, u32[]{:S(2)}, u32[]{:S(2)}) %collective-permute-start.12) | collective-permute-done | bytes 1048608 | tf_op jit(solution)/shard_map/ppermute | solution.py:30
  56.3 3.4 %collective-permute-done.13 = bf16[1024,512]{1,0:T(8,128)(2,1)} collective-permute-done((bf16[1024,512]{1,0:T(8,128)(2,1)S(1)}, bf16[1024,512]{1,0:T(8,128)(2,1)}, u32[]{:S(2)}, u32[]{:S(2)}) %collective-permute-start.13) | collective-permute-done | bytes 1048608 | tf_op jit(solution)/shard_map/ppermute | solution.py:30
  59.7 12.6 %collective-permute-start.17 = (bf16[1024,512]{1,0:T(8,128)(2,1)S(1)}, bf16[1024,512]{1,0:T(8,128)(2,1)}, u32[]{:S(2)}, u32[]{:S(2)}) collective-permute-start(bf16[1024,512]{1,0:T(8,128)(2,1)S(1)} %fusion.refs_0_), channel_id=1, source_target_pairs={{0,1},{1,0},{2,3},{3,2},{4,5},{5,4},{6,7},{7,6},{8,9},{9,8},{10,11... | collective-permute-start | bytes 3145736 | tf_op jit(solution)/shard_map/ppermute | solution.py:30
  72.3 3.8 %collective-permute-start.9 = (bf16[1024,256]{1,0:T(8,128)(2,1)}, bf16[1024,256]{1,0:T(8,128)(2,1)}, u32[]{:S(2)}, u32[]{:S(2)}) collective-permute-start(bf16[1024,256]{1,0:T(8,128)(2,1)} %constant_dynamic-slice_fusion.1.refs_0_), channel_id=1, source_target_pairs={{0,6},{1,7},{2,0},{3,1},{4,2},{5,3},{6,4},{7,5},{8,14},{9,15},{10,... | collective-permute-start | bytes 1572872 | tf_op jit(solution)/shard_map/ppermute | solution.py:30
  76.1 1.7 broadcast_select_fusion
  77.8 0.9 constant_dynamic-slice_fusion.refs_4_
  79.0 2.0 %collective-permute-start.16 = (bf16[1024,256]{1,0:T(8,128)(2,1)}, bf16[1024,256]{1,0:T(8,128)(2,1)}, u32[]{:S(2)}, u32[]{:S(2)}) collective-permute-start(bf16[1024,256]{1,0:T(8,128)(2,1)} %constant_dynamic-slice_fusion.refs_4_), channel_id=1, source_target_pairs={{0,2},{1,3},{2,4},{3,5},{4,6},{5,7},{6,0},{7,1},{8,10},{9,11},{10,... | collective-permute-start | bytes 1572872 | tf_op jit(solution)/shard_map/ppermute | solution.py:30
  81.0 2.2 %collective-permute-done.9.refs_1_ = bf16[1024,256]{1,0:T(8,128)(2,1)} collective-permute-done((bf16[1024,256]{1,0:T(8,128)(2,1)}, bf16[1024,256]{1,0:T(8,128)(2,1)}, u32[]{:S(2)}, u32[]{:S(2)}) %collective-permute-start.9) | collective-permute-done | bytes 524320 | tf_op jit(solution)/shard_map/ppermute | solution.py:30
  83.1 11.2 %collective-permute-done.14.refs_5_ = bf16[1024,256]{1,0:T(8,128)(2,1)} collective-permute-done((bf16[1024,256]{1,0:T(8,128)(2,1)}, bf16[1024,256]{1,0:T(8,128)(2,1)}, u32[]{:S(2)}, u32[]{:S(2)}) %collective-permute-start.14) | collective-permute-done | bytes 524320 | tf_op jit(solution)/shard_map/ppermute | solution.py:30
  94.4 0.9 collective-permute-done.16.refs_7_
  95.3 2.2 %copy-done.3 = bf16[2048,1024]{1,0:T(8,128)(2,1)S(1)} copy-done((bf16[2048,1024]{1,0:T(8,128)(2,1)S(1)}, bf16[2048,1024]{1,0:T(8,128)(2,1)}, u32[]{:S(2)}) %copy-start.3) | copy-done | bytes 4194328
  97.5 3.2 %open_rows_kernel.1 = (bf16[4,2048,256]{2,1,0:T(8,128)(2,1)S(1)}, bf16[4,2048,256]{2,1,0:T(8,128)(2,1)S(1)}) custom-call(bf16[1024,256]{1,0:T(8,128)(2,1)} %constant_dynamic-slice_fusion.1.refs_0_, bf16[1024,256]{1,0:T(8,128)(2,1)} %collective-permute-done.9.refs_1_, bf16[1024,256]{1,0:T(8,128)(2,1)} %collective-permute-done.10.refs_2_, ...), custom_call_target="tpu_custom_call" | custom-call | tf_op jit(solution)/shard_map/open_rows_kernel/pallas_call | solution.py:159
  100.7 3.0 %open_columns_kernel.1 = (bf16[2048,1024]{1,0:T(8,128)(2,1)S(1)}, bf16[2048,1024]{1,0:T(8,128)(2,1)S(1)}) custom-call(s32[1]{0:T(128)} %bitcast.15.zh, bf16[1024,512]{1,0:T(8,128)(2,1)S(1)} %fusion.refs_0_, bf16[1024,512]{1,0:T(8,128)(2,1)} %collective-permute-done.17.refs_1_, bf16[1024,512]{1,0:T(8,128)(2,1)S(1)} %get-tuple-element.44.refs_2_, ...), custom_call_target="tpu_custom_call" | custom-call | tf_op jit(solution)/shard_map/open_columns_kernel/pallas_call | solution.py:159
  103.7 1.3 convolution_bitcast_fusion.6
  105.0 1.3 convolution_bitcast_fusion.7
  106.3 0.6 copy-done.10
  106.9 1.2 fusion.12
  108.2 3.9 %convolution_bitcast_fusion.4 = f32[1,256,1024]{2,1,0:T(8,128)S(1)} fusion(bf16[2048,1024]{1,0:T(8,128)(2,1)} %copy-done.10, bf16[4,2048,256]{2,1,0:T(8,128)(2,1)} %copy-done.5, s32[]{:T(128)S(6)} %select_n.188), kind=kOutput, calls=%fused_computation.24 | convolution fusion | flops 1073741824 | bytes 6291460 | tf_op jit(solution)/shard_map/dot_general | solution.py:170
  112.2 2.9 %convolution_bitcast_fusion.5 = f32[1,256,1024]{2,1,0:T(8,128)S(1)} fusion(bf16[2048,1024]{1,0:T(8,128)(2,1)S(1)} %copy-done.7, bf16[4,2048,256]{2,1,0:T(8,128)(2,1)} %copy-done.4, s32[]{:T(128)S(6)} %select_n.188), kind=kOutput, calls=%fused_computation.25 | convolution fusion | flops 1073741824 | bytes 6291460 | tf_op jit(solution)/shard_map/dot_general | solution.py:170
  115.1 1.2 fusion.9
  116.6 3.9 %convolution_bitcast_fusion.2 = f32[1,256,1024]{2,1,0:T(8,128)S(1)} fusion(bf16[2048,1024]{1,0:T(8,128)(2,1)} %copy-done.10, bf16[4,2048,256]{2,1,0:T(8,128)(2,1)} %copy-done.5, s32[]{:T(128)S(6)} %select_n.193), kind=kOutput, calls=%fused_computation.22 | convolution fusion | flops 1073741824 | bytes 6291460 | tf_op jit(solution)/shard_map/dot_general | solution.py:170
  120.6 2.5 %convolution_bitcast_fusion.3 = f32[1,256,1024]{2,1,0:T(8,128)S(1)} fusion(bf16[2048,1024]{1,0:T(8,128)(2,1)S(1)} %copy-done.8, bf16[4,2048,256]{2,1,0:T(8,128)(2,1)} %copy-done.4, s32[]{:T(128)S(6)} %select_n.193), kind=kOutput, calls=%fused_computation.23 | convolution fusion | flops 1073741824 | bytes 6291460 | tf_op jit(solution)/shard_map/dot_general | solution.py:170
  123.1 1.1 fusion.6
  124.3 3.9 %convolution_bitcast_fusion = f32[1,256,1024]{2,1,0:T(8,128)S(1)} fusion(bf16[2048,1024]{1,0:T(8,128)(2,1)} %copy-done.10, bf16[4,2048,256]{2,1,0:T(8,128)(2,1)} %copy-done.5, s32[]{:T(128)S(6)} %select_n.198), kind=kOutput, calls=%fused_computation.20 | convolution fusion | flops 1073741824 | bytes 6291460 | tf_op jit(solution)/shard_map/dot_general | solution.py:170
  128.3 2.7 %convolution_bitcast_fusion.1 = f32[1,256,1024]{2,1,0:T(8,128)S(1)} fusion(bf16[2048,1024]{1,0:T(8,128)(2,1)S(1)} %copy-done.9, bf16[4,2048,256]{2,1,0:T(8,128)(2,1)} %copy-done.4, s32[]{:T(128)S(6)} %select_n.198), kind=kOutput, calls=%fused_computation.21 | convolution fusion | flops 1073741824 | bytes 6291460 | tf_op jit(solution)/shard_map/dot_general | solution.py:170
  131.6 1.6 fusion.14
  133.3 3.3 %collective-permute-start.19 = (bf16[2,256,512]{2,1,0:T(8,128)(2,1)S(1)}, bf16[2,256,512]{2,1,0:T(8,128)(2,1)S(1)}, u32[]{:S(2)}, u32[]{:S(2)}) collective-permute-start(bf16[2,256,512]{2,1,0:T(8,128)(2,1)S(1)} %pad_maximum_fusion.1), channel_id=1, source_target_pairs={{0,32},{1,33},{2,34},{3,35},{4,36},{5,37},{6,38},{7,39},{8,40},{9,... | collective-permute-start | bytes 1572872 | tf_op jit(solution)/shard_map/ppermute | solution.py:30
  136.6 1.4 fusion.11
  138.2 0.7 collective-permute-start.21
  139.0 1.4 fusion.8
  140.6 2.6 %collective-permute-start.23 = (bf16[2,256,512]{2,1,0:T(8,128)(2,1)S(1)}, bf16[2,256,512]{2,1,0:T(8,128)(2,1)S(1)}, u32[]{:S(2)}, u32[]{:S(2)}) collective-permute-start(bf16[2,256,512]{2,1,0:T(8,128)(2,1)S(1)} %pad_maximum_fusion.3), channel_id=1, source_target_pairs={{0,48},{1,49},{2,50},{3,51},{4,52},{5,53},{6,54},{7,55},{8,56},{9,... | collective-permute-start | bytes 1572872 | tf_op jit(solution)/shard_map/ppermute | solution.py:30
  143.2 6.5 %collective-permute-done.19 = bf16[2,256,512]{2,1,0:T(8,128)(2,1)S(1)} collective-permute-done((bf16[2,256,512]{2,1,0:T(8,128)(2,1)S(1)}, bf16[2,256,512]{2,1,0:T(8,128)(2,1)S(1)}, u32[]{:S(2)}, u32[]{:S(2)}) %collective-permute-start.19) | collective-permute-done | bytes 524320 | tf_op jit(solution)/shard_map/ppermute | solution.py:30
  149.7 10.3 %collective-permute-done.21 = bf16[2,256,512]{2,1,0:T(8,128)(2,1)S(1)} collective-permute-done((bf16[2,256,512]{2,1,0:T(8,128)(2,1)S(1)}, bf16[2,256,512]{2,1,0:T(8,128)(2,1)S(1)}, u32[]{:S(2)}, u32[]{:S(2)}) %collective-permute-start.21) | collective-permute-done | bytes 524320 | tf_op jit(solution)/shard_map/ppermute | solution.py:30
  161.0 1.9 %collective-permute-start.25 = (f32[256,512]{1,0:T(8,128)S(1)}, f32[256,512]{1,0:T(8,128)S(1)}, u32[]{:S(2)}, u32[]{:S(2)}) collective-permute-start(f32[256,512]{1,0:T(8,128)S(1)} %fusion.33), channel_id=1, source_target_pairs={{0,0},{1,16},{2,2},{3,18},{4,4},{5,20},{6,6},{7,22},{8,1},{9,17},{... | collective-permute-start | bytes 1572872 | tf_op jit(solution)/shard_map/ppermute | solution.py:30
  162.9 15.4 %collective-permute-done.25 = f32[256,512]{1,0:T(8,128)S(1)} collective-permute-done((f32[256,512]{1,0:T(8,128)S(1)}, f32[256,512]{1,0:T(8,128)S(1)}, u32[]{:S(2)}, u32[]{:S(2)}) %collective-permute-start.25) | collective-permute-done | bytes 524320 | tf_op jit(solution)/shard_map/ppermute | solution.py:30
  178.3 0.8 copy.26
  (97 shorter events, 6.0 us)
Async XLA Ops:
  1.0 8.5 %collective-permute-start = (f32[32,512]{1,0:T(8,128)S(1)}, f32[32,512]{1,0:T(8,128)S(1)}, u32[]{:S(2)}, u32[]{:S(2)}) collective-permute-start(f32[32,512]{1,0:T(8,128)S(1)} %maximum_maximum_fusion.value), channel_id=1, source_target_pairs={{0,1},{1,0},{2,3},{3,2},{4,5},{5,4},{6,7},{7,6},{8,9},{9,8},{10,11... | collective-permute-start | bytes 196616 | tf_op jit(solution)/shard_map/ppermute | solution.py:30
  7.6 9.6 %collective-permute-start.4 = (f32[32,1024]{1,0:T(8,128)S(1)}, f32[32,1024]{1,0:T(8,128)S(1)}, u32[]{:S(2)}, u32[]{:S(2)}) collective-permute-start(f32[32,1024]{1,0:T(8,128)S(1)} %fusion.1), channel_id=1, source_target_pairs={{0,1},{1,0},{2,3},{3,2},{4,5},{5,4},{6,7},{7,6},{8,9},{9,8},{10,11... | collective-permute-start | bytes 393224 | tf_op jit(solution)/shard_map/ppermute | solution.py:30
  11.3 9.3 %collective-permute-start.3 = (f32[2,32,512]{2,1,0:T(8,128)S(1)}, f32[2,32,512]{2,1,0:T(8,128)S(1)}, u32[]{:S(2)}, u32[]{:S(2)}) collective-permute-start(f32[2,32,512]{2,1,0:T(8,128)S(1)} %pad_maximum_fusion.4), channel_id=1, source_target_pairs={{0,2},{1,3},{2,4},{3,5},{4,6},{5,7},{6,0},{7,1},{8,10},{9,11},{10,... | collective-permute-start | bytes 393224 | tf_op jit(solution)/shard_map/ppermute | solution.py:30
  12.8 9.4 %collective-permute-start.2 = (f32[2,32,512]{2,1,0:T(8,128)S(1)}, f32[2,32,512]{2,1,0:T(8,128)S(1)}, u32[]{:S(2)}, u32[]{:S(2)}) collective-permute-start(f32[2,32,512]{2,1,0:T(8,128)S(1)} %pad_maximum_fusion.4), channel_id=1, source_target_pairs={{0,4},{1,5},{2,6},{3,7},{4,0},{5,1},{6,2},{7,3},{8,12},{9,13},{10,... | collective-permute-start | bytes 393224 | tf_op jit(solution)/shard_map/ppermute | solution.py:30
  15.6 7.6 %collective-permute-start.1 = (f32[2,32,512]{2,1,0:T(8,128)S(1)}, f32[2,32,512]{2,1,0:T(8,128)S(1)}, u32[]{:S(2)}, u32[]{:S(2)}) collective-permute-start(f32[2,32,512]{2,1,0:T(8,128)S(1)} %pad_maximum_fusion.4), channel_id=1, source_target_pairs={{0,6},{1,7},{2,0},{3,1},{4,2},{5,3},{6,4},{7,5},{8,14},{9,15},{10,... | collective-permute-start | bytes 393224 | tf_op jit(solution)/shard_map/ppermute | solution.py:30
  17.2 11.7 %collective-permute-start.5 = (f32[32,1024]{1,0:T(8,128)S(1)}, f32[32,1024]{1,0:T(8,128)S(1)}, u32[]{:S(2)}, u32[]{:S(2)}) collective-permute-start(f32[32,1024]{1,0:T(8,128)S(1)} %add.202), channel_id=1, source_target_pairs={{0,4},{1,5},{2,6},{3,7},{4,0},{5,1},{6,2},{7,3},{8,12},{9,13},{10,... | collective-permute-start | bytes 393224 | tf_op jit(solution)/shard_map/ppermute | solution.py:30
  17.8 11.1 %collective-permute-start.6 = (f32[32,1024]{1,0:T(8,128)S(1)}, f32[32,1024]{1,0:T(8,128)S(1)}, u32[]{:S(2)}, u32[]{:S(2)}) collective-permute-start(f32[32,1024]{1,0:T(8,128)S(1)} %add.202), channel_id=1, source_target_pairs={{0,6},{1,7},{2,0},{3,1},{4,2},{5,3},{6,4},{7,5},{8,14},{9,15},{10,... | collective-permute-start | bytes 393224 | tf_op jit(solution)/shard_map/ppermute | solution.py:30
  20.6 8.4 %collective-permute-start.7 = (f32[32,1024]{1,0:T(8,128)S(1)}, f32[32,1024]{1,0:T(8,128)S(1)}, u32[]{:S(2)}, u32[]{:S(2)}) collective-permute-start(f32[32,1024]{1,0:T(8,128)S(1)} %add.202), channel_id=1, source_target_pairs={{0,2},{1,3},{2,4},{3,5},{4,6},{5,7},{6,0},{7,1},{8,10},{9,11},{10,... | collective-permute-start | bytes 393224 | tf_op jit(solution)/shard_map/ppermute | solution.py:30
  29.3 6.4 %collective-permute-start.8 = (f32[32,1024]{1,0:T(8,128)S(1)}, f32[32,1024]{1,0:T(8,128)S(1)}, u32[]{:S(2)}, u32[]{:S(2)}) collective-permute-start(f32[32,1024]{1,0:T(8,128)S(1)} %fusion.37.value), channel_id=1, source_target_pairs={{0,65},{1,64},{2,67},{3,66},{4,69},{5,68},{6,71},{7,70},{8,73},{9,... | collective-permute-start | bytes 393224 | tf_op jit(solution)/shard_map/ppermute | solution.py:30
  35.7 20.6 %collective-permute-start.12 = (bf16[1024,512]{1,0:T(8,128)(2,1)S(1)}, bf16[1024,512]{1,0:T(8,128)(2,1)}, u32[]{:S(2)}, u32[]{:S(2)}) collective-permute-start(bf16[1024,512]{1,0:T(8,128)(2,1)S(1)} %fusion.refs_0_), channel_id=1, source_target_pairs={{0,65},{1,64},{2,67},{3,66},{4,69},{5,68},{6,71},{7,70},{8,73},{9,... | collective-permute-start | bytes 3145736 | tf_op jit(solution)/shard_map/ppermute | solution.py:30
  37.0 22.8 %collective-permute-start.13 = (bf16[1024,512]{1,0:T(8,128)(2,1)S(1)}, bf16[1024,512]{1,0:T(8,128)(2,1)}, u32[]{:S(2)}, u32[]{:S(2)}) collective-permute-start(bf16[1024,512]{1,0:T(8,128)(2,1)S(1)} %fusion.refs_0_), channel_id=1, source_target_pairs={{0,64},{1,65},{2,66},{3,67},{4,68},{5,69},{6,70},{7,71},{8,72},{9,... | collective-permute-start | bytes 3145736 | tf_op jit(solution)/shard_map/ppermute | solution.py:30
  38.8 39.9 %collective-permute-start.10 = (bf16[1024,256]{1,0:T(8,128)(2,1)}, bf16[1024,256]{1,0:T(8,128)(2,1)}, u32[]{:S(2)}, u32[]{:S(2)}) collective-permute-start(bf16[1024,256]{1,0:T(8,128)(2,1)} %constant_dynamic-slice_fusion.1.refs_0_), channel_id=1, source_target_pairs={{0,4},{1,5},{2,6},{3,7},{4,0},{5,1},{6,2},{7,3},{8,12},{9,13},{10,... | collective-permute-start | bytes 1572872 | tf_op jit(solution)/shard_map/ppermute | solution.py:30
  41.2 37.7 %collective-permute-start.11 = (bf16[1024,256]{1,0:T(8,128)(2,1)}, bf16[1024,256]{1,0:T(8,128)(2,1)}, u32[]{:S(2)}, u32[]{:S(2)}) collective-permute-start(bf16[1024,256]{1,0:T(8,128)(2,1)} %constant_dynamic-slice_fusion.1.refs_0_), channel_id=1, source_target_pairs={{0,2},{1,3},{2,4},{3,5},{4,6},{5,7},{6,0},{7,1},{8,10},{9,11},{10,... | collective-permute-start | bytes 1572872 | tf_op jit(solution)/shard_map/ppermute | solution.py:30
  50.1 2.0 %copy-start = (bf16[2048,1024]{1,0:T(8,128)(2,1)}, bf16[2048,1024]{1,0:T(8,128)(2,1)S(1)}, u32[]{:S(2)}) copy-start(bf16[2048,1024]{1,0:T(8,128)(2,1)S(1)} %get-tuple-element.30.refs_4_) | copy-start | bytes 12582916
  52.0 2.0 %copy-start.2 = (bf16[2048,1024]{1,0:T(8,128)(2,1)}, bf16[2048,1024]{1,0:T(8,128)(2,1)S(1)}, u32[]{:S(2)}) copy-start(bf16[2048,1024]{1,0:T(8,128)(2,1)S(1)} %get-tuple-element.27.refs_8_) | copy-start | bytes 12582916
  59.7 41.0 %collective-permute-start.17 = (bf16[1024,512]{1,0:T(8,128)(2,1)S(1)}, bf16[1024,512]{1,0:T(8,128)(2,1)}, u32[]{:S(2)}, u32[]{:S(2)}) collective-permute-start(bf16[1024,512]{1,0:T(8,128)(2,1)S(1)} %fusion.refs_0_), channel_id=1, source_target_pairs={{0,1},{1,0},{2,3},{3,2},{4,5},{5,4},{6,7},{7,6},{8,9},{9,8},{10,11... | collective-permute-start | bytes 3145736 | tf_op jit(solution)/shard_map/ppermute | solution.py:30
  72.3 10.8 %collective-permute-start.9 = (bf16[1024,256]{1,0:T(8,128)(2,1)}, bf16[1024,256]{1,0:T(8,128)(2,1)}, u32[]{:S(2)}, u32[]{:S(2)}) collective-permute-start(bf16[1024,256]{1,0:T(8,128)(2,1)} %constant_dynamic-slice_fusion.1.refs_0_), channel_id=1, source_target_pairs={{0,6},{1,7},{2,0},{3,1},{4,2},{5,3},{6,4},{7,5},{8,14},{9,15},{10,... | collective-permute-start | bytes 1572872 | tf_op jit(solution)/shard_map/ppermute | solution.py:30
  78.7 15.7 %collective-permute-start.14 = (bf16[1024,256]{1,0:T(8,128)(2,1)}, bf16[1024,256]{1,0:T(8,128)(2,1)}, u32[]{:S(2)}, u32[]{:S(2)}) collective-permute-start(bf16[1024,256]{1,0:T(8,128)(2,1)} %constant_dynamic-slice_fusion.refs_4_), channel_id=1, source_target_pairs={{0,6},{1,7},{2,0},{3,1},{4,2},{5,3},{6,4},{7,5},{8,14},{9,15},{10,... | collective-permute-start | bytes 1572872 | tf_op jit(solution)/shard_map/ppermute | solution.py:30
  78.7 15.7 %collective-permute-start.15 = (bf16[1024,256]{1,0:T(8,128)(2,1)}, bf16[1024,256]{1,0:T(8,128)(2,1)}, u32[]{:S(2)}, u32[]{:S(2)}) collective-permute-start(bf16[1024,256]{1,0:T(8,128)(2,1)} %constant_dynamic-slice_fusion.refs_4_), channel_id=1, source_target_pairs={{0,4},{1,5},{2,6},{3,7},{4,0},{5,1},{6,2},{7,3},{8,12},{9,13},{10,... | collective-permute-start | bytes 1572872 | tf_op jit(solution)/shard_map/ppermute | solution.py:30
  79.0 16.3 %collective-permute-start.16 = (bf16[1024,256]{1,0:T(8,128)(2,1)}, bf16[1024,256]{1,0:T(8,128)(2,1)}, u32[]{:S(2)}, u32[]{:S(2)}) collective-permute-start(bf16[1024,256]{1,0:T(8,128)(2,1)} %constant_dynamic-slice_fusion.refs_4_), channel_id=1, source_target_pairs={{0,2},{1,3},{2,4},{3,5},{4,6},{5,7},{6,0},{7,1},{8,10},{9,11},{10,... | collective-permute-start | bytes 1572872 | tf_op jit(solution)/shard_map/ppermute | solution.py:30
  81.0 19.8 %copy-start.1 = (bf16[2048,1024]{1,0:T(8,128)(2,1)S(1)}, bf16[2048,1024]{1,0:T(8,128)(2,1)}, u32[]{:S(2)}) copy-start(bf16[2048,1024]{1,0:T(8,128)(2,1)} %copy-done) | copy-start | bytes 12582916
  95.3 2.2 %copy-start.3 = (bf16[2048,1024]{1,0:T(8,128)(2,1)S(1)}, bf16[2048,1024]{1,0:T(8,128)(2,1)}, u32[]{:S(2)}) copy-start(bf16[2048,1024]{1,0:T(8,128)(2,1)} %copy-done.2) | copy-start | bytes 12582916
  100.7 3.0 %copy-start.5 = (bf16[4,2048,256]{2,1,0:T(8,128)(2,1)}, bf16[4,2048,256]{2,1,0:T(8,128)(2,1)S(1)}, u32[]{:S(2)}) copy-start(bf16[4,2048,256]{2,1,0:T(8,128)(2,1)S(1)} %get-tuple-element.32) | copy-start | bytes 12582916
  100.7 4.3 %copy-start.4 = (bf16[4,2048,256]{2,1,0:T(8,128)(2,1)}, bf16[4,2048,256]{2,1,0:T(8,128)(2,1)S(1)}, u32[]{:S(2)}) copy-start(bf16[4,2048,256]{2,1,0:T(8,128)(2,1)S(1)} %get-tuple-element.28) | copy-start | bytes 12582916
  103.7 2.6 %copy-start.6 = (bf16[2048,1024]{1,0:T(8,128)(2,1)}, bf16[2048,1024]{1,0:T(8,128)(2,1)S(1)}, u32[]{:S(2)}) copy-start(bf16[2048,1024]{1,0:T(8,128)(2,1)S(1)} %get-tuple-element.31) | copy-start | bytes 12582916
  103.7 3.2 %copy-start.10 = (bf16[2048,1024]{1,0:T(8,128)(2,1)}, bf16[2048,1024]{1,0:T(8,128)(2,1)S(1)}, u32[]{:S(2)}) copy-start(bf16[2048,1024]{1,0:T(8,128)(2,1)S(1)} %get-tuple-element.33) | copy-start | bytes 12582916
  105.0 3.1 %copy-start.15 = (f32[1,256,1024]{2,1,0:T(8,128)}, f32[1,256,1024]{2,1,0:T(8,128)S(1)}, u32[]{:S(2)}) copy-start(f32[1,256,1024]{2,1,0:T(8,128)S(1)} %convolution_bitcast_fusion.6) | copy-start | bytes 3145732
  106.9 1.3 copy-start.17
  108.1 23.5 %collective-permute-start.18 = (f32[2,256,512]{2,1,0:T(8,128)}, f32[2,256,512]{2,1,0:T(8,128)}, u32[]{:S(2)}, u32[]{:S(2)}) collective-permute-start(f32[2,256,512]{2,1,0:T(8,128)} %fusion.12), channel_id=1, source_target_pairs={{0,8},{1,9},{2,10},{3,11},{4,12},{5,13},{6,14},{7,15},{8,0},{9,1},... | collective-permute-start | bytes 3145736 | tf_op jit(solution)/shard_map/ppermute | solution.py:30
  108.2 3.9 %copy-start.7 = (bf16[2048,1024]{1,0:T(8,128)(2,1)S(1)}, bf16[2048,1024]{1,0:T(8,128)(2,1)}, u32[]{:S(2)}) copy-start(bf16[2048,1024]{1,0:T(8,128)(2,1)} %copy-done.6) | copy-start | bytes 12582916
  112.2 4.1 %copy-start.11 = (f32[1,256,1024]{2,1,0:T(8,128)}, f32[1,256,1024]{2,1,0:T(8,128)S(1)}, u32[]{:S(2)}) copy-start(f32[1,256,1024]{2,1,0:T(8,128)S(1)} %convolution_bitcast_fusion.4) | copy-start | bytes 3145732
  115.1 1.5 copy-start.13
  116.3 20.3 %collective-permute-start.20 = (f32[2,256,512]{2,1,0:T(8,128)}, f32[2,256,512]{2,1,0:T(8,128)}, u32[]{:S(2)}, u32[]{:S(2)}) collective-permute-start(f32[2,256,512]{2,1,0:T(8,128)} %fusion.9), channel_id=1, source_target_pairs={{0,8},{1,9},{2,10},{3,11},{4,12},{5,13},{6,14},{7,15},{8,0},{9,1},... | collective-permute-start | bytes 3145736 | tf_op jit(solution)/shard_map/ppermute | solution.py:30
  116.6 3.9 %copy-start.8 = (bf16[2048,1024]{1,0:T(8,128)(2,1)S(1)}, bf16[2048,1024]{1,0:T(8,128)(2,1)}, u32[]{:S(2)}) copy-start(bf16[2048,1024]{1,0:T(8,128)(2,1)} %copy-done.6) | copy-start | bytes 12582916
  124.2 14.8 %collective-permute-start.22 = (f32[2,256,512]{2,1,0:T(8,128)}, f32[2,256,512]{2,1,0:T(8,128)}, u32[]{:S(2)}, u32[]{:S(2)}) collective-permute-start(f32[2,256,512]{2,1,0:T(8,128)} %fusion.6), channel_id=1, source_target_pairs={{0,8},{1,9},{2,10},{3,11},{4,12},{5,13},{6,14},{7,15},{8,0},{9,1},... | collective-permute-start | bytes 3145736 | tf_op jit(solution)/shard_map/ppermute | solution.py:30
  124.3 3.9 %copy-start.9 = (bf16[2048,1024]{1,0:T(8,128)(2,1)S(1)}, bf16[2048,1024]{1,0:T(8,128)(2,1)}, u32[]{:S(2)}) copy-start(bf16[2048,1024]{1,0:T(8,128)(2,1)} %copy-done.6) | copy-start | bytes 12582916
  128.3 3.3 %copy-start.16 = (f32[1,256,1024]{2,1,0:T(8,128)S(1)}, f32[1,256,1024]{2,1,0:T(8,128)}, u32[]{:S(2)}) copy-start(f32[1,256,1024]{2,1,0:T(8,128)} %copy-done.15) | copy-start | bytes 3145732
  128.3 3.3 %copy-start.18 = (f32[1,256,1024]{2,1,0:T(8,128)S(1)}, f32[1,256,1024]{2,1,0:T(8,128)}, u32[]{:S(2)}) copy-start(f32[1,256,1024]{2,1,0:T(8,128)} %copy-done.17) | copy-start | bytes 3145732
  131.1 5.5 %copy-start.12 = (f32[1,256,1024]{2,1,0:T(8,128)S(1)}, f32[1,256,1024]{2,1,0:T(8,128)}, u32[]{:S(2)}) copy-start(f32[1,256,1024]{2,1,0:T(8,128)} %copy-done.11) | copy-start | bytes 3145732
  131.1 5.5 %copy-start.14 = (f32[1,256,1024]{2,1,0:T(8,128)S(1)}, f32[1,256,1024]{2,1,0:T(8,128)}, u32[]{:S(2)}) copy-start(f32[1,256,1024]{2,1,0:T(8,128)} %copy-done.13) | copy-start | bytes 3145732
  131.1 12.1 %collective-permute-start.24 = (f32[2,256,512]{2,1,0:T(8,128)S(1)}, f32[2,256,512]{2,1,0:T(8,128)S(1)}, u32[]{:S(2)}, u32[]{:S(2)}) collective-permute-start(f32[2,256,512]{2,1,0:T(8,128)S(1)} %fusion.2), channel_id=1, source_target_pairs={{0,8},{1,9},{2,10},{3,11},{4,12},{5,13},{6,14},{7,15},{8,0},{9,1},... | collective-permute-start | bytes 3145736 | tf_op jit(solution)/shard_map/ppermute | solution.py:30
  133.3 16.4 %collective-permute-start.19 = (bf16[2,256,512]{2,1,0:T(8,128)(2,1)S(1)}, bf16[2,256,512]{2,1,0:T(8,128)(2,1)S(1)}, u32[]{:S(2)}, u32[]{:S(2)}) collective-permute-start(bf16[2,256,512]{2,1,0:T(8,128)(2,1)S(1)} %pad_maximum_fusion.1), channel_id=1, source_target_pairs={{0,32},{1,33},{2,34},{3,35},{4,36},{5,37},{6,38},{7,39},{8,40},{9,... | collective-permute-start | bytes 1572872 | tf_op jit(solution)/shard_map/ppermute | solution.py:30
  138.2 21.8 %collective-permute-start.21 = (bf16[2,256,512]{2,1,0:T(8,128)(2,1)S(1)}, bf16[2,256,512]{2,1,0:T(8,128)(2,1)S(1)}, u32[]{:S(2)}, u32[]{:S(2)}) collective-permute-start(bf16[2,256,512]{2,1,0:T(8,128)(2,1)S(1)} %pad_maximum_fusion.2), channel_id=1, source_target_pairs={{0,16},{1,17},{2,18},{3,19},{4,20},{5,21},{6,22},{7,23},{8,24},{9,... | collective-permute-start | bytes 1572872 | tf_op jit(solution)/shard_map/ppermute | solution.py:30
  140.6 19.9 %collective-permute-start.23 = (bf16[2,256,512]{2,1,0:T(8,128)(2,1)S(1)}, bf16[2,256,512]{2,1,0:T(8,128)(2,1)S(1)}, u32[]{:S(2)}, u32[]{:S(2)}) collective-permute-start(bf16[2,256,512]{2,1,0:T(8,128)(2,1)S(1)} %pad_maximum_fusion.3), channel_id=1, source_target_pairs={{0,48},{1,49},{2,50},{3,51},{4,52},{5,53},{6,54},{7,55},{8,56},{9,... | collective-permute-start | bytes 1572872 | tf_op jit(solution)/shard_map/ppermute | solution.py:30
  161.0 17.4 %collective-permute-start.25 = (f32[256,512]{1,0:T(8,128)S(1)}, f32[256,512]{1,0:T(8,128)S(1)}, u32[]{:S(2)}, u32[]{:S(2)}) collective-permute-start(f32[256,512]{1,0:T(8,128)S(1)} %fusion.33), channel_id=1, source_target_pairs={{0,0},{1,16},{2,2},{3,18},{4,4},{5,20},{6,6},{7,22},{8,1},{9,17},{... | collective-permute-start | bytes 1572872 | tf_op jit(solution)/shard_map/ppermute | solution.py:30

commit v2 on v0

v2 whole, which is shorter than its diff:
```python
import functools

import jax
import jax.numpy as jnp
from jax import lax
from jax.experimental import pallas as pl
from jax.experimental.pallas import tpu as pltpu
from jax.sharding import PartitionSpec as P

AXES = ("snp", "samp")
HIGH = lax.Precision.HIGHEST
MISSING = 4.0
PAD = 32
TILE = 256


def decode(snp, samp):
    return samp // 2, (snp // 2) % 4, samp % 2, snp // 8, snp % 2


def encode(x, y, zh, zl, c):
    return ((zl * 4 + y) * 2 + c) * 8 + x * 2 + zh


def pairs(where):
    return [(s * 8 + j, encode(*where(*decode(s, j)))) for s in range(16) for j in range(8)]


def move(value, where):
    return lax.ppermute(value, AXES, pairs(where))


def from_x(value, d):
    return move(value, lambda x, y, zh, zl, c: ((x - d) % 4, y, zh, zl, c))


def from_z(value, d):
    def where(x, y, zh, zl, c):
        z = (zh * 2 + zl - d) % 4
        return x, y, z // 2, z % 2, c

    return move(value, where)


def rows_at(y, zh):
    return zh * ((y % 2) * 2 + y // 2) + (1 - zh) * (y + y // 2 * (1 - y % 2 * 2))


def to_owner(value):
    def where(x, y, zh, zl, c):
        xi = rows_at(y, zh)
        return x, (xi % 2) * 2 + zh, c, xi // 2, zl

    return move(value, where)


LEFT = (0, 0, 1, 0, 2, 1)
RIGHT = (0, 1, 0, 2, 0, 1)


def terms_kernel(order, value, out):
    for k, part in enumerate(split_terms(value[...], order)):
        out[k * PAD : (k + 1) * PAD, :] = part


def terms(value, order):
    rows, columns = value.shape
    return pl.pallas_call(
        functools.partial(terms_kernel, order),
        out_shape=jax.ShapeDtypeStruct((rows * len(order), columns), jnp.bfloat16),
        compiler_params=pltpu.CompilerParams(vmem_limit_bytes=4 << 20),
        name="terms",
    )(value)


def frequencies(coef6, design6):
    fitted = lax.dot_general(coef6, design6, (((0,), (0,)), ((), ())), preferred_element_type=jnp.float32)
    return jnp.clip(0.5 * fitted, 0.02, 0.98)


def split_terms(a, order):
    parts = []
    for _ in range(3):
        parts.append(a.astype(jnp.bfloat16))
        a = a - parts[-1].astype(jnp.float32)
    return [parts[part] for part in order]


def clipped_spread(fitted):
    freq = jnp.clip(0.5 * fitted, 0.02, 0.98)
    square = freq * (1.0 - freq)
    return (square * lax.rsqrt(square)).astype(jnp.bfloat16)


def place(x, y, z, c):
    return ((z % 2) * 4 + y) * 2 + c, x * 2 + z // 2


def kinship_kernel(
    code, near6, right6, coef, out,
    across, near_in, far_in, coef_far, far6, col_resid, col_spread, row_resid, row_spread,
    product, flipped, y_out, y_in, send_sem, recv_sem,
):
    x, y, zh, zl, c = decode(lax.axis_index("snp"), lax.axis_index("samp"))
    z = zh * 2 + zl
    length, here = code.shape
    half = here // 2
    mine = pl.ds(pl.multiple_of(zl * half, half), half)

    to_x = [None] + [place((x + 4 - d) % 4, y, z, c) for d in (1, 2, 3)]
    to_y = [None] + [place(x, (y + d) % 4, z, c) for d in (1, 2, 3)]
    to_z = [None] + [place(x, y, (z + 4 - d) % 4, c) for d in (1, 2, 3)]
    core = place(x, y, z, 1 - c)

    def copy(n, source, target, device):
        return pltpu.make_async_remote_copy(
            src_ref=source,
            dst_ref=target,
            send_sem=send_sem.at[n],
            recv_sem=recv_sem.at[n],
            device_id=device,
            device_id_type=pl.DeviceIdType.MESH,
        )

    barrier = pltpu.get_barrier_semaphore()
    peers = to_x[1:] + to_y[1:] + to_z[1:] + [core]
    for peer in peers:
        pl.semaphore_signal(barrier, inc=1, device_id=peer, device_id_type=pl.DeviceIdType.MESH)
    pl.semaphore_wait(barrier, len(peers))

    far_coef = copy(0, coef, coef_far, to_z[1])
    from_up = copy(1, code, across.at[0], to_z[1])
    from_down = copy(2, code, across.at[1], to_z[3])
    from_two = copy(3, code, across.at[2], to_z[2])
    near = [copy(3 + d, code.at[:, mine], near_in.at[d - 1], to_x[d]) for d in (1, 2, 3)]
    far = [copy(6 + d, across.at[zl, :, mine], far_in.at[d - 1], to_x[d]) for d in (1, 2, 3)]
    far_coef.start()
    from_up.start()
    from_down.start()
    for one in near:
        one.start()

    def column_spreads(left, base):
        @pl.loop(0, length // TILE)
        def _(k):
            flat = left[:, pl.ds(pl.multiple_of(k * TILE, TILE), TILE)].T
            at = pl.ds(pl.multiple_of(base + k * TILE, TILE), TILE)
            for n in range(0, 2 * here, TILE):
                fitted = jnp.dot(flat, right6[:, n : n + TILE], preferred_element_type=jnp.float32)
                col_spread[at, n : n + TILE] = clipped_spread(fitted)

    def row_spreads(left, base):
        for d in range(4):
            first = 2 * here + d * half
            flat = right6[:, first : first + half].T

            @pl.loop(0, length // TILE)
            def _(k):
                fitted = jnp.dot(
                    flat, left[:, pl.ds(pl.multiple_of(k * TILE, TILE), TILE)], preferred_element_type=jnp.float32
                )
                row_spread[d, :, pl.ds(pl.multiple_of(base + k * TILE, TILE), TILE)] = clipped_spread(fitted)

    def open_columns(load, base, block):
        lanes = pl.ds(pl.multiple_of(block * here, here), here)

        @pl.loop(0, length // TILE)
        def _(k):
            value = load(pl.ds(pl.multiple_of(k * TILE, TILE), TILE))
            at = pl.ds(pl.multiple_of(base + k * TILE, TILE), TILE)
            zero = jnp.zeros_like(value)
            col_resid[at, lanes] = jnp.where(value < 3.0, value, zero)
            col_spread[at, lanes] = jnp.where(value < 3.0, col_spread[at, lanes], zero)

    def open_rows(load, base, d):
        @pl.loop(0, length // TILE)
        def _(k):
            value = load(pl.ds(pl.multiple_of(k * TILE, TILE), TILE)).T
            at = pl.ds(pl.multiple_of(base + k * TILE, TILE), TILE)
            zero = jnp.zeros_like(value)
            row_resid[d, :, at] = jnp.where(value < 3.0, value, zero)
            row_spread[d, :, at] = jnp.where(value < 3.0, row_spread[d, :, at], zero)

    column_spreads(near6, 0)
    row_spreads(near6, 0)
    far_coef.wait_recv()
    for k, part in enumerate(split_terms(coef_far[...], LEFT)):
        far6[k * PAD : (k + 1) * PAD, :] = part
    column_spreads(far6, length)
    row_spreads(far6, length)
    open_columns(lambda at: code[at, :], 0, zh)
    open_rows(lambda at: code[at, mine], 0, 0)
    from_up.wait_recv()
    from_down.wait_recv()
    for one in far:
        one.start()
    from_two.start()
    open_columns(lambda at: across[zl, at, :], length, zh)
    open_columns(lambda at: across[1 - zl, at, :], length, 1 - zh)
    open_rows(lambda at: across[zl, at, mine], length, 0)
    for d in (1, 2, 3):
        near[d - 1].wait_recv()
        open_rows(lambda at: near_in[d - 1, at, :], 0, d)
    for d in (1, 3, 2):
        far[d - 1].wait_recv()
        open_rows(lambda at: far_in[d - 1, at, :], length, d)
    from_two.wait_recv()
    open_columns(lambda at: across[2, at, :], 0, 1 - zh)

    flips = [copy(10 + s, product.at[s, 1 - c], flipped.at[s], core) for s in range(4)]
    sends = [None] + [copy(13 + s, y_out.at[s - 1], y_in.at[s - 1], to_y[s]) for s in (1, 2, 3)]

    def multiply(step):
        d = (rows_at((y + step) % 4, zh) + 4 - x) % 4
        for which, (left, right) in enumerate(((row_resid, col_resid), (row_spread, col_spread))):

            @pl.loop(0, 2 * here // TILE)
            def _(k):
                at = pl.ds(pl.multiple_of(k * TILE, TILE), TILE)
                inner = pl.ds(pl.multiple_of(k % 2 * TILE, TILE), TILE)
                product[step, k // 2, which, :, inner] = jnp.dot(
                    left[d], right[:, at], preferred_element_type=jnp.float32
                )

        flips[step].start()

    STRIP = 64

    def merge(step):
        flips[step].wait_recv()

        @pl.loop(0, half // STRIP)
        def _(k):
            at = pl.ds(pl.multiple_of(k * STRIP, STRIP), STRIP)
            numer = product[step, c, 0, at, :] + flipped[step, 0, at, :]
            denom = product[step, c, 1, at, :] + flipped[step, 1, at, :]
            low = denom.astype(jnp.bfloat16)
            y_out[step - 1, 0, at, :] = (numer * (low.astype(jnp.float32) / denom)).astype(jnp.bfloat16)
            y_out[step - 1, 1, at, :] = low

        sends[step].start()

    multiply(2)
    multiply(1)
    merge(2)
    multiply(3)
    merge(1)
    multiply(0)
    merge(3)
    flips[0].wait_recv()
    for s in (1, 3, 2):
        sends[s].wait_recv()

    @pl.loop(0, half // STRIP)
    def _(k):
        at = pl.ds(pl.multiple_of(k * STRIP, STRIP), STRIP)
        sums = []
        for which in range(2):
            total = product[0, c, which, at, :] + flipped[0, which, at, :]
            for s in range(3):
                total = total + y_in[s, which, at, :].astype(jnp.float32)
            sums.append(total)
        out[at, :] = sums[0] / (4.0 * sums[1])

    for one in [far_coef, from_up, from_down, from_two] + near + far + flips + sends[1:]:
        one.wait_send()


def kinship_blocks(code, near6, right6, coef):
    length, here = code.shape
    half = here // 2
    wide = lambda *shape: pltpu.VMEM(shape, jnp.float32)
    narrow = lambda *shape: pltpu.VMEM(shape, jnp.bfloat16)
    return pl.pallas_call(
        kinship_kernel,
        in_specs=[VMEM] * 4,
        out_specs=VMEM,
        out_shape=jax.ShapeDtypeStruct((half, here), jnp.float32),
        scratch_shapes=[
            narrow(3, length, here),
            narrow(3, length, half),
            narrow(3, length, half),
            wide(*coef.shape),
            narrow(*near6.shape),
            narrow(2 * length, 2 * here),
            narrow(2 * length, 2 * here),
            narrow(4, half, 2 * length),
            narrow(4, half, 2 * length),
            wide(4, 2, 2, half, here),
            wide(4, 2, half, here),
            narrow(3, 2, half, here),
            narrow(3, 2, half, here),
            pltpu.SemaphoreType.DMA((17,)),
            pltpu.SemaphoreType.DMA((17,)),
        ],
        compiler_params=pltpu.CompilerParams(
            collective_id=0, has_side_effects=True, vmem_limit_bytes=52 << 20
        ),
        name="kinship_blocks",
    )(code, near6, right6, coef)


VMEM = pl.BlockSpec(memory_space=pltpu.VMEM)


def body(genotypes, pcs):
    x, y, zh, zl, c = decode(lax.axis_index("snp"), lax.axis_index("samp"))
    here = genotypes.shape[1]
    half = here // 2
    count = pcs.shape[0] + 1
    design = jnp.concatenate([jnp.ones((1, here), jnp.float32), pcs, jnp.zeros((PAD - count, here), jnp.float32)], axis=0)
    design_zh = jnp.stack([design, from_z(design, 2)])
    designs = [design_zh] + [from_x(design_zh, d) for d in (1, 2, 3)]
    observed = genotypes >= 0.0
    dosage = jnp.where(observed, genotypes, 0.0)
    cross = lax.dot_general(design, dosage, (((1,), (1,)), ((), ())), precision=HIGH)
    cross = cross + from_z(cross, 2)
    cross = (cross + from_x(cross, 2)) + (from_x(cross, 1) + from_x(cross, 3))
    total = None
    for d in designs:
        for k in range(2):
            part = lax.dot_general(d[k], d[k], (((1,), (1,)), ((), ())), precision=HIGH)
            total = part if total is None else total + part
    factor = jnp.linalg.cholesky(total[:count, :count])
    inverse = jax.scipy.linalg.cho_solve((factor, True), jnp.eye(count, dtype=jnp.float32))
    inverse = jnp.pad(inverse, ((0, PAD - count), (0, PAD - count)))
    coef = jnp.dot(inverse, cross, precision=HIGH)

    def in_order(a, b):
        return jnp.concatenate([jnp.where(zh == 0, a, b), jnp.where(zh == 0, b, a)], axis=1)

    def my_half(value):
        return lax.dynamic_slice(value, (0, zl * half), (value.shape[0], half))

    own6 = terms(design, RIGHT)
    all6 = terms(jnp.concatenate([in_order(*designs[0])] + [my_half(d[0]) for d in designs], axis=1), RIGHT)
    near6 = terms(coef, LEFT)
    freq = frequencies(near6, own6)
    code = jnp.where(observed, dosage - 2.0 * freq, MISSING).astype(jnp.bfloat16)
    return to_owner(kinship_blocks(code, near6, all6, coef))


def solution(mesh):
    in_specs = (P("snp", "samp"), P(None, "samp"))
    out_specs = P("snp", "samp")
    return jax.shard_map(body, mesh=mesh, in_specs=in_specs, out_specs=out_specs, check_vma=False)
```

time: 184 us -> 138 us (0.75)
  Pallas kernels: 23.2 us -> 89.1 us
  waiting for transfers between devices: 57.3 us -> 15.6 us
  other arithmetic: 41 us -> 5.93 us
  starting transfers between devices: 39.8 us -> 15.8 us
  matrix products: 19.8 us -> 8.53 us
    pallas_call x3 -> x1, Pallas kernels: 23 us -> 88.9 us  [kinship_blocks(): pl.pallas_call(kinship_kernel, in_specs=[VMEM] * 4, out_specs=VMEM, out_s...]
    ppermute x26 -> x9, waiting for transfers between devices: 57.3 us -> 15.6 us  [move(): return lax.ppermute(value, AXES, pairs(where))]
    concatenate x3 -> x0, other arithmetic: 26.3 us -> none  [the longest x1 23.5 us: body(): jnp.concatenate([jnp.concatenate(near_rows, axis=1), jnp.concatenate(far_...]
    ppermute x26 -> x9, starting transfers between devices: 39.8 us -> 15.8 us  [move(): return lax.ppermute(value, AXES, pairs(where))]
    dot_general x8 -> x0, matrix products: 10.4 us -> none  [gram(): lax.dot_general(a, b, (((0,), (0,)), ((), ())), preferred_element_type=jn...]
    select_n x3 -> x0, other arithmetic: 5.04 us -> none  [the longest x2 3.82 us: in_order(): jnp.where(zh == 0, a, b)]
  transfers between devices with their start and end apart: 26 -> 9, of which waited for: 7 -> 1; matrix products, arithmetic and copies ran while one was open for 25% -> 8% of each run, Pallas kernels for 12% -> 0%
where the time goes in v2:
time: 138 us; the launch traced here: 136 us
  Pallas kernels  89.1 us (65%)
  starting transfers between devices  15.8 us (11%)
  waiting for transfers between devices  15.6 us (11%)
  matrix products  8.53 us (6%)
  other arithmetic  5.93 us (4%)
    pallas_call x1, Pallas kernels, kinship_blocks(): pl.pallas_call(kinship_kernel, in_specs=[VMEM] * 4, out_specs=VMEM, out_s...  88.9 us
    ppermute x9, starting transfers between devices, move(): return lax.ppermute(value, AXES, pairs(where))  15.8 us
    ppermute x9, waiting for transfers between devices, move(): return lax.ppermute(value, AXES, pairs(where))  15.6 us
    dot_general x1, matrix products, body(): lax.dot_general(design, dosage, (((1,), (1,)), ((), ())), precision=HIGH)  3.62 us
  transfers between devices with their start and end apart: 9, of which 1 were waited for; matrix products, arithmetic and copies ran while one was open for 8% of the time, Pallas kernels for 0%

profile of v2, /device:TPU:32, one launch (start us, length us, event | category | flops | bytes accessed | tf_op | source)
XLA Modules:
  0.0 136.4 jit_solution(18375072679456640705)
XLA Ops:
  0.0 0.0 copy-start.1
  0.0 0.1 pad.9.clone
  0.1 0.9 maximum_maximum_fusion.value
  1.0 3.1 %collective-permute-start = (f32[32,512]{1,0:T(8,128)S(1)}, f32[32,512]{1,0:T(8,128)S(1)}, u32[]{:S(2)}, u32[]{:S(2)}) collective-permute-start(f32[32,512]{1,0:T(8,128)S(1)} %maximum_maximum_fusion.value), channel_id=1, source_target_pairs={{0,1},{1,0},{2,3},{3,2},{4,5},{5,4},{6,7},{7,6},{8,9},{9,8},{10,11... | collective-permute-start | bytes 196616 | tf_op jit(solution)/shard_map/ppermute | solution.py:30
  4.0 3.6 %fusion.1 = f32[32,1024]{1,0:T(8,128)S(1)} fusion(f32[1024,512]{1,0:T(8,128)} %param.2, f32[20,512]{1,0:T(8,128)} %param.3, f32[32]{0:T(128)S(1)} %pad.9.clone, f32[32]{0:T(128)S(1)} %pad.7.clone), kind=kOutput, calls=%fused_computation.3 | convolution fusion | flops 202407936 | bytes 2269440 | tf_op jit(solution)/shard_map/dot_general | solution.py:316
  7.6 0.6 collective-permute-start.4
  8.3 0.0 copy-done.1
  8.3 0.3 fusion.29
  8.6 0.0 collective-permute-done
  8.6 0.1 select_dynamic-update-slice_fusion.1
  8.7 0.1 select_dynamic-update-slice_fusion
  8.8 0.0 copy-start
  8.8 1.6 %collective-permute-start.3 = (f32[2,32,512]{2,1,0:T(8,128)S(1)}, f32[2,32,512]{2,1,0:T(8,128)S(1)}, u32[]{:S(2)}, u32[]{:S(2)}) collective-permute-start(f32[2,32,512]{2,1,0:T(8,128)S(1)} %pad_maximum_fusion), channel_id=1, source_target_pairs={{0,2},{1,3},{2,4},{3,5},{4,6},{5,7},{6,0},{7,1},{8,10},{9,11},{10,... | collective-permute-start | bytes 393224 | tf_op jit(solution)/shard_map/ppermute | solution.py:30
  10.4 2.7 %collective-permute-start.2 = (f32[2,32,512]{2,1,0:T(8,128)S(1)}, f32[2,32,512]{2,1,0:T(8,128)S(1)}, u32[]{:S(2)}, u32[]{:S(2)}) collective-permute-start(f32[2,32,512]{2,1,0:T(8,128)S(1)} %pad_maximum_fusion), channel_id=1, source_target_pairs={{0,4},{1,5},{2,6},{3,7},{4,0},{5,1},{6,2},{7,3},{8,12},{9,13},{10,... | collective-permute-start | bytes 393224 | tf_op jit(solution)/shard_map/ppermute | solution.py:30
  13.1 1.4 %collective-permute-start.1 = (f32[2,32,512]{2,1,0:T(8,128)S(1)}, f32[2,32,512]{2,1,0:T(8,128)S(1)}, u32[]{:S(2)}, u32[]{:S(2)}) collective-permute-start(f32[2,32,512]{2,1,0:T(8,128)S(1)} %pad_maximum_fusion), channel_id=1, source_target_pairs={{0,6},{1,7},{2,0},{3,1},{4,2},{5,3},{6,4},{7,5},{8,14},{9,15},{10,... | collective-permute-start | bytes 393224 | tf_op jit(solution)/shard_map/ppermute | solution.py:30
  14.6 0.2 convolution_add_fusion
  14.8 0.0 collective-permute-done.4
  14.8 1.0 collective-permute-start.7
  15.8 2.4 %collective-permute-start.6 = (f32[32,1024]{1,0:T(8,128)S(1)}, f32[32,1024]{1,0:T(8,128)S(1)}, u32[]{:S(2)}, u32[]{:S(2)}) collective-permute-start(f32[32,1024]{1,0:T(8,128)S(1)} %add.69), channel_id=1, source_target_pairs={{0,6},{1,7},{2,0},{3,1},{4,2},{5,3},{6,4},{7,5},{8,14},{9,15},{10,... | collective-permute-start | bytes 393224 | tf_op jit(solution)/shard_map/ppermute | solution.py:30
  18.1 0.0 collective-permute-done.3
  18.1 1.2 collective-permute-start.5
  19.3 0.2 fusion.10
  19.5 0.2 fusion.7
  19.7 0.0 collective-permute-done.2
  19.8 0.2 fusion.12
  20.0 0.2 fusion.8
  20.2 0.0 collective-permute-done.1
  20.2 0.2 fusion.14
  20.4 0.2 fusion.9
  20.6 0.1 copy.11
  20.7 1.9 %cholesky.17 = f32[21,21]{1,0:T(8,128)S(1)} custom-call(f32[21,21]{1,0:T(8,128)S(1)} %fusion.22), custom_call_target="Cholesky" | custom-call | tf_op jit(solution)/shard_map/jit(cholesky)/cholesky | solution.py:324
  22.6 0.6 compare_reduce_fusion
  23.3 0.6 fusion.17
  23.9 1.6 %custom-call.10 = f32[1,21,21]{1,2,0:T(8,128)S(1)} custom-call(f32[1,21,21]{2,1,0:T(8,128)S(1)} %fusion.17), custom_call_target="InvertDiagBlocksLowerTriangular" | custom-call | tf_op jit(solution)/shard_map/jit(_cho_solve)/triangular_solve | solution.py:325
  25.5 0.2 fusion.20
  25.9 0.1 terms.5.right6
  26.0 0.1 fusion.18
  26.1 0.0 collective-permute-done.7
  26.1 0.0 collective-permute-done.6
  26.1 0.0 collective-permute-done.5
  26.1 1.2 fusion.3.value.coef
  27.3 0.0 copy-done
  27.4 1.8 %fusion.code = bf16[1024,512]{1,0:T(8,128)(2,1)} fusion(f32[1024,512]{1,0:T(8,128)S(1)} %copy-done, bf16[192,1024]{1,0:T(8,128)(2,1)S(1)} %terms.3.near6, bf16[192,512]{1,0:T(8,128)(2,1)S(1)} %terms.4), kind=kOutput, calls=%fused_computation.2 | convolution fusion | flops 205520896 | bytes 3735552 | tf_op jit(solution)/shard_map/dot_general | solution.py:77
  29.1 88.9 %kinship_blocks.1 = f32[256,512]{1,0:T(8,128)S(1)} custom-call(bf16[1024,512]{1,0:T(8,128)(2,1)} %fusion.code, bf16[192,1024]{1,0:T(8,128)(2,1)S(1)} %terms.3.near6, bf16[192,2048]{1,0:T(8,128)(2,1)S(1)} %terms.5.right6, f32[32,1024]{1,0:T(8,128)S(1)} %fusion.3.value.coef), custom_call_target="tpu_custom_call" | custom-call | tf_op jit(solution)/shard_map/kinship_blocks/pallas_call | solution.py:274
  118.1 1.9 %collective-permute-start.8 = (f32[256,512]{1,0:T(8,128)S(1)}, f32[256,512]{1,0:T(8,128)S(1)}, u32[]{:S(2)}, u32[]{:S(2)}) collective-permute-start(f32[256,512]{1,0:T(8,128)S(1)} %kinship_blocks.1), channel_id=1, source_target_pairs={{0,0},{1,16},{2,2},{3,18},{4,4},{5,20},{6,6},{7,22},{8,1},{9,17},{... | collective-permute-start | bytes 1572872 | tf_op jit(solution)/shard_map/ppermute | solution.py:30
  120.0 15.6 %collective-permute-done.8 = f32[256,512]{1,0:T(8,128)S(1)} collective-permute-done((f32[256,512]{1,0:T(8,128)S(1)}, f32[256,512]{1,0:T(8,128)S(1)}, u32[]{:S(2)}, u32[]{:S(2)}) %collective-permute-start.8) | collective-permute-done | bytes 524320 | tf_op jit(solution)/shard_map/ppermute | solution.py:30
  135.6 0.8 copy.26
  (16 shorter events, 0.2 us)
Async XLA Ops:
  0.0 8.3 %copy-start.1 = (f32[20,512]{1,0:T(8,128)S(1)}, f32[20,512]{1,0:T(8,128)}, u32[]{:S(2)}) copy-start(f32[20,512]{1,0:T(8,128)} %param.3) | copy-start | bytes 122884
  1.0 7.7 %collective-permute-start = (f32[32,512]{1,0:T(8,128)S(1)}, f32[32,512]{1,0:T(8,128)S(1)}, u32[]{:S(2)}, u32[]{:S(2)}) collective-permute-start(f32[32,512]{1,0:T(8,128)S(1)} %maximum_maximum_fusion.value), channel_id=1, source_target_pairs={{0,1},{1,0},{2,3},{3,2},{4,5},{5,4},{6,7},{7,6},{8,9},{9,8},{10,11... | collective-permute-start | bytes 196616 | tf_op jit(solution)/shard_map/ppermute | solution.py:30
  7.6 7.1 %collective-permute-start.4 = (f32[32,1024]{1,0:T(8,128)S(1)}, f32[32,1024]{1,0:T(8,128)S(1)}, u32[]{:S(2)}, u32[]{:S(2)}) collective-permute-start(f32[32,1024]{1,0:T(8,128)S(1)} %fusion.1), channel_id=1, source_target_pairs={{0,1},{1,0},{2,3},{3,2},{4,5},{5,4},{6,7},{7,6},{8,9},{9,8},{10,11... | collective-permute-start | bytes 393224 | tf_op jit(solution)/shard_map/ppermute | solution.py:30
  8.8 18.5 %copy-start = (f32[1024,512]{1,0:T(8,128)S(1)}, f32[1024,512]{1,0:T(8,128)}, u32[]{:S(2)}) copy-start(f32[1024,512]{1,0:T(8,128)} %param.2) | copy-start | bytes 6291460
  8.8 9.3 %collective-permute-start.3 = (f32[2,32,512]{2,1,0:T(8,128)S(1)}, f32[2,32,512]{2,1,0:T(8,128)S(1)}, u32[]{:S(2)}, u32[]{:S(2)}) collective-permute-start(f32[2,32,512]{2,1,0:T(8,128)S(1)} %pad_maximum_fusion), channel_id=1, source_target_pairs={{0,2},{1,3},{2,4},{3,5},{4,6},{5,7},{6,0},{7,1},{8,10},{9,11},{10,... | collective-permute-start | bytes 393224 | tf_op jit(solution)/shard_map/ppermute | solution.py:30
  10.4 9.3 %collective-permute-start.2 = (f32[2,32,512]{2,1,0:T(8,128)S(1)}, f32[2,32,512]{2,1,0:T(8,128)S(1)}, u32[]{:S(2)}, u32[]{:S(2)}) collective-permute-start(f32[2,32,512]{2,1,0:T(8,128)S(1)} %pad_maximum_fusion), channel_id=1, source_target_pairs={{0,4},{1,5},{2,6},{3,7},{4,0},{5,1},{6,2},{7,3},{8,12},{9,13},{10,... | collective-permute-start | bytes 393224 | tf_op jit(solution)/shard_map/ppermute | solution.py:30
  13.1 7.0 %collective-permute-start.1 = (f32[2,32,512]{2,1,0:T(8,128)S(1)}, f32[2,32,512]{2,1,0:T(8,128)S(1)}, u32[]{:S(2)}, u32[]{:S(2)}) collective-permute-start(f32[2,32,512]{2,1,0:T(8,128)S(1)} %pad_maximum_fusion), channel_id=1, source_target_pairs={{0,6},{1,7},{2,0},{3,1},{4,2},{5,3},{6,4},{7,5},{8,14},{9,15},{10,... | collective-permute-start | bytes 393224 | tf_op jit(solution)/shard_map/ppermute | solution.py:30
  14.8 11.3 %collective-permute-start.7 = (f32[32,1024]{1,0:T(8,128)S(1)}, f32[32,1024]{1,0:T(8,128)S(1)}, u32[]{:S(2)}, u32[]{:S(2)}) collective-permute-start(f32[32,1024]{1,0:T(8,128)S(1)} %add.69), channel_id=1, source_target_pairs={{0,2},{1,3},{2,4},{3,5},{4,6},{5,7},{6,0},{7,1},{8,10},{9,11},{10,... | collective-permute-start | bytes 393224 | tf_op jit(solution)/shard_map/ppermute | solution.py:30
  15.8 10.3 %collective-permute-start.6 = (f32[32,1024]{1,0:T(8,128)S(1)}, f32[32,1024]{1,0:T(8,128)S(1)}, u32[]{:S(2)}, u32[]{:S(2)}) collective-permute-start(f32[32,1024]{1,0:T(8,128)S(1)} %add.69), channel_id=1, source_target_pairs={{0,6},{1,7},{2,0},{3,1},{4,2},{5,3},{6,4},{7,5},{8,14},{9,15},{10,... | collective-permute-start | bytes 393224 | tf_op jit(solution)/shard_map/ppermute | solution.py:30
  18.1 8.0 %collective-permute-start.5 = (f32[32,1024]{1,0:T(8,128)S(1)}, f32[32,1024]{1,0:T(8,128)}, u32[]{:S(2)}, u32[]{:S(2)}) collective-permute-start(f32[32,1024]{1,0:T(8,128)S(1)} %add.69), channel_id=1, source_target_pairs={{0,4},{1,5},{2,6},{3,7},{4,0},{5,1},{6,2},{7,3},{8,12},{9,13},{10,... | collective-permute-start | bytes 393224 | tf_op jit(solution)/shard_map/ppermute | solution.py:30
  118.1 17.5 %collective-permute-start.8 = (f32[256,512]{1,0:T(8,128)S(1)}, f32[256,512]{1,0:T(8,128)S(1)}, u32[]{:S(2)}, u32[]{:S(2)}) collective-permute-start(f32[256,512]{1,0:T(8,128)S(1)} %kinship_blocks.1), channel_id=1, source_target_pairs={{0,0},{1,16},{2,2},{3,18},{4,4},{5,20},{6,6},{7,22},{8,1},{9,17},{... | collective-permute-start | bytes 1572872 | tf_op jit(solution)/shard_map/ppermute | solution.py:30

commit v3 on v2

--- a/solution.py
+++ b/solution.py
@@ -44,14 +44,6 @@
 
 def rows_at(y, zh):
     return zh * ((y % 2) * 2 + y // 2) + (1 - zh) * (y + y // 2 * (1 - y % 2 * 2))
-
-
-def to_owner(value):
-    def where(x, y, zh, zl, c):
-        xi = rows_at(y, zh)
-        return x, (xi % 2) * 2 + zh, c, xi // 2, zl
-
-    return move(value, where)
 
 
 LEFT = (0, 0, 1, 0, 2, 1)
@@ -99,13 +91,15 @@
 def kinship_kernel(
     code, near6, right6, coef, out,
     across, near_in, far_in, coef_far, far6, col_resid, col_spread, row_resid, row_spread,
-    product, flipped, y_out, y_in, send_sem, recv_sem,
+    product, flipped, y_out, y_in, done, send_sem, recv_sem,
 ):
     x, y, zh, zl, c = decode(lax.axis_index("snp"), lax.axis_index("samp"))
     z = zh * 2 + zl
     length, here = code.shape
     half = here // 2
     mine = pl.ds(pl.multiple_of(zl * half, half), half)
+    other = pl.ds(pl.multiple_of((1 - zl) * half, half), half)
+    top, bottom = pl.ds(0, length // 2), pl.ds(length // 2, length // 2)
 
     to_x = [None] + [place((x + 4 - d) % 4, y, z, c) for d in (1, 2, 3)]
     to_y = [None] + [place(x, (y + d) % 4, z, c) for d in (1, 2, 3)]
@@ -122,22 +116,44 @@
             device_id_type=pl.DeviceIdType.MESH,
         )
 
+    xi = rows_at(y, zh)
+    target = place(x, xi % 2 * 2 + zh, c * 2 + xi // 2, zl)
+    source = place(x, rows_at(zl * 2 + y // 2, y % 2), y % 2 * 2 + c, zh)
+    here_snp, here_samp = place(x, y, z, c)
+    stays = jnp.logical_and(target[0] == here_snp, target[1] == here_samp)
+    leaves = jnp.logical_not(stays)
+
     barrier = pltpu.get_barrier_semaphore()
-    peers = to_x[1:] + to_y[1:] + to_z[1:] + [core]
+    peers = to_x[1:] + to_y[1:] + [to_z[1], to_z[3], core]
     for peer in peers:
         pl.semaphore_signal(barrier, inc=1, device_id=peer, device_id_type=pl.DeviceIdType.MESH)
-    pl.semaphore_wait(barrier, len(peers))
+
+    @pl.when(leaves)
+    def _():
+        for peer in (target, source):
+            pl.semaphore_signal(barrier, inc=1, device_id=peer, device_id_type=pl.DeviceIdType.MESH)
+
+    pl.semaphore_wait(barrier, len(peers) + 2 * leaves.astype(jnp.int32))
 
     far_coef = copy(0, coef, coef_far, to_z[1])
-    from_up = copy(1, code, across.at[0], to_z[1])
-    from_down = copy(2, code, across.at[1], to_z[3])
-    from_two = copy(3, code, across.at[2], to_z[2])
-    near = [copy(3 + d, code.at[:, mine], near_in.at[d - 1], to_x[d]) for d in (1, 2, 3)]
-    far = [copy(6 + d, across.at[zl, :, mine], far_in.at[d - 1], to_x[d]) for d in (1, 2, 3)]
-    far_coef.start()
-    from_up.start()
-    from_down.start()
-    for one in near:
+    up_mine = copy(1, code.at[:, other], across.at[0, :, other], to_z[1])
+    down_mine = copy(2, code.at[:, other], across.at[1, :, other], to_z[3])
+    up_other = copy(3, code.at[:, mine], across.at[0, :, mine], to_z[1])
+    down_other = copy(4, code.at[:, mine], across.at[1, :, mine], to_z[3])
+    two_up = copy(5, across.at[0, :, mine], across.at[2, :, mine], to_z[1])
+    two_down = copy(6, across.at[1, :, other], across.at[2, :, other], to_z[3])
+
+    def along_x(n, first, into):
+        return [
+            copy(n, first, into.at[0], to_x[1]),
+            copy(n + 1, first, into.at[2], to_x[3]),
+            copy(n + 2, into.at[0, top], into.at[1, top], to_x[1]),
+            copy(n + 3, into.at[2, bottom], into.at[1, bottom], to_x[3]),
+        ]
+
+    near = along_x(7, code.at[:, mine], near_in)
+    far = along_x(11, across.at[zl, :, mine], far_in)
+    for one in (up_mine, down_mine, near[0], near[1], far_coef, up_other, down_other):
         one.start()
 
     def column_spreads(left, base):
@@ -190,25 +206,45 @@
     row_spreads(far6, length)
     open_columns(lambda at: code[at, :], 0, zh)
     open_rows(lambda at: code[at, mine], 0, 0)
-    from_up.wait_recv()
-    from_down.wait_recv()
-    for one in far:
+    up_mine.wait_recv()
+    down_mine.wait_recv()
+    for one in (far[0], far[1], two_up):
         one.start()
-    from_two.start()
+    near[0].wait_recv()
+    near[2].start()
+    near[1].wait_recv()
+    near[3].start()
+    open_rows(lambda at: across[zl, at, mine], length, 0)
+    open_rows(lambda at: near_in[0, at, :], 0, 1)
+    open_rows(lambda at: near_in[2, at, :], 0, 3)
+    down_other.wait_recv()
+    two_down.start()
+    far[0].wait_recv()
+    far[2].start()
+    far[1].wait_recv()
+    far[3].start()
+    up_other.wait_recv()
     open_columns(lambda at: across[zl, at, :], length, zh)
     open_columns(lambda at: across[1 - zl, at, :], length, 1 - zh)
-    open_rows(lambda at: across[zl, at, mine], length, 0)
-    for d in (1, 2, 3):
-        near[d - 1].wait_recv()
-        open_rows(lambda at: near_in[d - 1, at, :], 0, d)
-    for d in (1, 3, 2):
-        far[d - 1].wait_recv()
-        open_rows(lambda at: far_in[d - 1, at, :], length, d)
-    from_two.wait_recv()
+    open_rows(lambda at: far_in[0, at, :], length, 1)
+    open_rows(lambda at: far_in[2, at, :], length, 3)
+    near[2].wait_recv()
+    near[3].wait_recv()
+    open_rows(lambda at: near_in[1, at, :], 0, 2)
+    two_up.wait_recv()
+    two_down.wait_recv()
     open_columns(lambda at: across[2, at, :], 0, 1 - zh)
-
-    flips = [copy(10 + s, product.at[s, 1 - c], flipped.at[s], core) for s in range(4)]
-    sends = [None] + [copy(13 + s, y_out.at[s - 1], y_in.at[s - 1], to_y[s]) for s in (1, 2, 3)]
+    far[2].wait_recv()
+    far[3].wait_recv()
+    open_rows(lambda at: far_in[1, at, :], length, 2)
+
+    strips = [pl.ds(t * (half // 2), half // 2) for t in range(2)]
+    flips = [copy(15 + s, product.at[s, 1 - c], flipped.at[s], core) for s in range(4)]
+    sends = [None] + [
+        [copy(17 + s * 2 + t, y_out.at[s - 1, :, strips[t]], y_in.at[s - 1, :, strips[t]], to_y[s]) for t in range(2)]
+        for s in (1, 2, 3)
+    ]
+    last = [copy(25 + t, done.at[strips[t]], out.at[strips[t]], target) for t in range(2)]
 
     def multiply(step):
         d = (rows_at((y + step) % 4, zh) + 4 - x) % 4
@@ -238,7 +274,8 @@
             y_out[step - 1, 0, at, :] = (numer * (low.astype(jnp.float32) / denom)).astype(jnp.bfloat16)
             y_out[step - 1, 1, at, :] = low
 
-        sends[step].start()
+        for one in sends[step]:
+            one.start()
 
     multiply(2)
     multiply(1)
@@ -248,22 +285,37 @@
     multiply(0)
     merge(3)
     flips[0].wait_recv()
-    for s in (1, 3, 2):
-        sends[s].wait_recv()
-
-    @pl.loop(0, half // STRIP)
-    def _(k):
-        at = pl.ds(pl.multiple_of(k * STRIP, STRIP), STRIP)
-        sums = []
-        for which in range(2):
-            total = product[0, c, which, at, :] + flipped[0, which, at, :]
-            for s in range(3):
-                total = total + y_in[s, which, at, :].astype(jnp.float32)
-            sums.append(total)
-        out[at, :] = sums[0] / (4.0 * sums[1])
-
-    for one in [far_coef, from_up, from_down, from_two] + near + far + flips + sends[1:]:
+    for t in range(2):
+        for s in (2, 1, 3):
+            sends[s][t].wait_recv()
+
+        @pl.loop(0, half // 2 // STRIP)
+        def _(k):
+            at = pl.ds(pl.multiple_of(t * (half // 2) + k * STRIP, STRIP), STRIP)
+            sums = []
+            for which in range(2):
+                total = product[0, c, which, at, :] + flipped[0, which, at, :]
+                for s in range(3):
+                    total = total + y_in[s, which, at, :].astype(jnp.float32)
+                sums.append(total)
+            done[at, :] = sums[0] / (4.0 * sums[1])
+
+        @pl.when(leaves)
+        def _():
+            last[t].start()
+
+    @pl.when(stays)
+    def _():
+        out[...] = done[...]
+
+    moved = [far_coef, up_mine, down_mine, up_other, down_other, two_up, two_down]
+    for one in moved + near + far + flips + sends[1] + sends[2] + sends[3]:
         one.wait_send()
+
+    @pl.when(leaves)
+    def _():
+        for one in last:
+            one.wait()
 
 
 def kinship_blocks(code, near6, right6, coef):
@@ -290,8 +342,9 @@
             wide(4, 2, half, here),
             narrow(3, 2, half, here),
             narrow(3, 2, half, here),
-            pltpu.SemaphoreType.DMA((17,)),
-            pltpu.SemaphoreType.DMA((17,)),
+            wide(half, here),
+            pltpu.SemaphoreType.DMA((27,)),
+            pltpu.SemaphoreType.DMA((27,)),
         ],
         compiler_params=pltpu.CompilerParams(
             collective_id=0, has_side_effects=True, vmem_limit_bytes=52 << 20
@@ -337,7 +390,7 @@
     near6 = terms(coef, LEFT)
     freq = frequencies(near6, own6)
     code = jnp.where(observed, dosage - 2.0 * freq, MISSING).astype(jnp.bfloat16)
-    return to_owner(kinship_blocks(code, near6, all6, coef))
+    return kinship_blocks(code, near6, all6, coef)
 
 
 def solution(mesh):

time: 138 us -> 128 us (0.928)
  the two profiles are of different devices: /device:TPU:32 before, /device:TPU:25 now
where the time goes in v3:
time: 128 us
  Pallas kernels  99.6 us (78%)
  starting transfers between devices  12.5 us (10%)
  matrix products  8.53 us (7%)
  other arithmetic  5.93 us (5%)
    pallas_call x1, Pallas kernels, kinship_blocks(): pl.pallas_call(kinship_kernel, in_specs=[VMEM] * 4, out_specs=VMEM, out_s...  99.4 us
    ppermute x8, starting transfers between devices, move(): return lax.ppermute(value, AXES, pairs(where))  12.5 us
    dot_general x1, matrix products, body(): lax.dot_general(design, dosage, (((1,), (1,)), ((), ())), precision=HIGH)  3.62 us
    another operation x3, other arithmetic, body(): factor = jnp.linalg.cholesky(total[:count, :count])  2.58 us
  transfers between devices with their start and end apart: 8, of which 0 were waited for; matrix products, arithmetic and copies ran while one was open for 8% of the time, Pallas kernels for 0%

profile of v3, /device:TPU:25, one launch (start us, length us, event | category | flops | bytes accessed | tf_op | source)
XLA Modules:
  0.0 128.0 jit_solution(1211322852901502680)
XLA Ops:
  0.0 0.0 copy-start.1
  0.0 0.1 pad.9.clone
  0.1 0.9 maximum_maximum_fusion.value
  1.0 3.7 %collective-permute-start = (f32[32,512]{1,0:T(8,128)S(1)}, f32[32,512]{1,0:T(8,128)S(1)}, u32[]{:S(2)}, u32[]{:S(2)}) collective-permute-start(f32[32,512]{1,0:T(8,128)S(1)} %maximum_maximum_fusion.value), channel_id=1, source_target_pairs={{0,1},{1,0},{2,3},{3,2},{4,5},{5,4},{6,7},{7,6},{8,9},{9,8},{10,11... | collective-permute-start | bytes 196616 | tf_op jit(solution)/shard_map/ppermute | solution.py:30
  4.6 3.6 %fusion.1 = f32[32,1024]{1,0:T(8,128)S(1)} fusion(f32[1024,512]{1,0:T(8,128)} %param.2, f32[20,512]{1,0:T(8,128)} %param.3, f32[32]{0:T(128)S(1)} %pad.9.clone, f32[32]{0:T(128)S(1)} %pad.7.clone), kind=kOutput, calls=%fused_computation.3 | convolution fusion | flops 202407936 | bytes 2269440 | tf_op jit(solution)/shard_map/dot_general | solution.py:369
  8.3 0.1 collective-permute-start.4
  8.4 0.0 copy-done.1
  8.4 0.3 fusion.29
  8.7 0.0 collective-permute-done
  8.7 0.1 select_dynamic-update-slice_fusion.1
  8.8 0.1 select_dynamic-update-slice_fusion
  8.9 0.0 copy-start
  8.9 1.3 collective-permute-start.3
  10.2 2.5 %collective-permute-start.2 = (f32[2,32,512]{2,1,0:T(8,128)S(1)}, f32[2,32,512]{2,1,0:T(8,128)S(1)}, u32[]{:S(2)}, u32[]{:S(2)}) collective-permute-start(f32[2,32,512]{2,1,0:T(8,128)S(1)} %pad_maximum_fusion), channel_id=1, source_target_pairs={{0,4},{1,5},{2,6},{3,7},{4,0},{5,1},{6,2},{7,3},{8,12},{9,13},{10,... | collective-permute-start | bytes 393224 | tf_op jit(solution)/shard_map/ppermute | solution.py:30
  12.7 1.2 collective-permute-start.1
  13.8 0.2 convolution_add_fusion
  14.0 0.0 collective-permute-done.4
  14.1 0.9 collective-permute-start.7
  15.0 1.9 %collective-permute-start.6 = (f32[32,1024]{1,0:T(8,128)S(1)}, f32[32,1024]{1,0:T(8,128)S(1)}, u32[]{:S(2)}, u32[]{:S(2)}) collective-permute-start(f32[32,1024]{1,0:T(8,128)S(1)} %add.69), channel_id=1, source_target_pairs={{0,6},{1,7},{2,0},{3,1},{4,2},{5,3},{6,4},{7,5},{8,14},{9,15},{10,... | collective-permute-start | bytes 393224 | tf_op jit(solution)/shard_map/ppermute | solution.py:30
  16.8 0.0 collective-permute-done.3
  16.8 1.1 collective-permute-start.5
  18.0 0.2 fusion.10
  18.2 0.2 fusion.7
  18.4 0.0 collective-permute-done.2
  18.4 0.2 fusion.12
  18.6 0.2 fusion.8
  18.8 0.0 collective-permute-done.1
  18.8 0.2 fusion.14
  19.0 0.2 fusion.9
  19.2 0.1 copy.11
  19.3 1.9 %cholesky.17 = f32[21,21]{1,0:T(8,128)S(1)} custom-call(f32[21,21]{1,0:T(8,128)S(1)} %fusion.22), custom_call_target="Cholesky" | custom-call | tf_op jit(solution)/shard_map/jit(cholesky)/cholesky | solution.py:377
  21.3 0.6 compare_reduce_fusion
  21.9 0.6 fusion.17
  22.6 1.6 %custom-call.10 = f32[1,21,21]{1,2,0:T(8,128)S(1)} custom-call(f32[1,21,21]{2,1,0:T(8,128)S(1)} %fusion.17), custom_call_target="InvertDiagBlocksLowerTriangular" | custom-call | tf_op jit(solution)/shard_map/jit(_cho_solve)/triangular_solve | solution.py:378
  24.2 0.2 fusion.20
  24.5 0.1 terms.5.right6
  24.6 0.1 fusion.18
  24.7 0.0 collective-permute-done.7
  24.7 0.0 collective-permute-done.6
  24.8 0.0 collective-permute-done.5
  24.8 1.2 fusion.3.value.coef
  26.0 0.0 copy-done
  26.0 1.8 %fusion.code = bf16[1024,512]{1,0:T(8,128)(2,1)} fusion(f32[1024,512]{1,0:T(8,128)S(1)} %copy-done, bf16[192,1024]{1,0:T(8,128)(2,1)S(1)} %terms.3.near6, bf16[192,512]{1,0:T(8,128)(2,1)S(1)} %terms.4), kind=kOutput, calls=%fused_computation.2 | convolution fusion | flops 205520896 | bytes 3735552 | tf_op jit(solution)/shard_map/dot_general | solution.py:69
  27.8 99.4 %kinship_blocks.1 = f32[256,512]{1,0:T(8,128)S(1)} custom-call(bf16[1024,512]{1,0:T(8,128)(2,1)} %fusion.code, bf16[192,1024]{1,0:T(8,128)(2,1)S(1)} %terms.3.near6, bf16[192,2048]{1,0:T(8,128)(2,1)S(1)} %terms.5.right6, f32[32,1024]{1,0:T(8,128)S(1)} %fusion.3.value.coef), custom_call_target="tpu_custom_call" | custom-call | tf_op jit(solution)/shard_map/kinship_blocks/pallas_call | solution.py:326
  127.2 0.8 copy.26
  (16 shorter events, 0.2 us)
Async XLA Ops:
  0.0 8.4 %copy-start.1 = (f32[20,512]{1,0:T(8,128)S(1)}, f32[20,512]{1,0:T(8,128)}, u32[]{:S(2)}) copy-start(f32[20,512]{1,0:T(8,128)} %param.3) | copy-start | bytes 122884
  1.0 7.8 %collective-permute-start = (f32[32,512]{1,0:T(8,128)S(1)}, f32[32,512]{1,0:T(8,128)S(1)}, u32[]{:S(2)}, u32[]{:S(2)}) collective-permute-start(f32[32,512]{1,0:T(8,128)S(1)} %maximum_maximum_fusion.value), channel_id=1, source_target_pairs={{0,1},{1,0},{2,3},{3,2},{4,5},{5,4},{6,7},{7,6},{8,9},{9,8},{10,11... | collective-permute-start | bytes 196616 | tf_op jit(solution)/shard_map/ppermute | solution.py:30
  8.3 5.8 %collective-permute-start.4 = (f32[32,1024]{1,0:T(8,128)S(1)}, f32[32,1024]{1,0:T(8,128)S(1)}, u32[]{:S(2)}, u32[]{:S(2)}) collective-permute-start(f32[32,1024]{1,0:T(8,128)S(1)} %fusion.1), channel_id=1, source_target_pairs={{0,1},{1,0},{2,3},{3,2},{4,5},{5,4},{6,7},{7,6},{8,9},{9,8},{10,11... | collective-permute-start | bytes 393224 | tf_op jit(solution)/shard_map/ppermute | solution.py:30
  8.9 17.1 %copy-start = (f32[1024,512]{1,0:T(8,128)S(1)}, f32[1024,512]{1,0:T(8,128)}, u32[]{:S(2)}) copy-start(f32[1024,512]{1,0:T(8,128)} %param.2) | copy-start | bytes 6291460
  8.9 7.9 %collective-permute-start.3 = (f32[2,32,512]{2,1,0:T(8,128)S(1)}, f32[2,32,512]{2,1,0:T(8,128)S(1)}, u32[]{:S(2)}, u32[]{:S(2)}) collective-permute-start(f32[2,32,512]{2,1,0:T(8,128)S(1)} %pad_maximum_fusion), channel_id=1, source_target_pairs={{0,2},{1,3},{2,4},{3,5},{4,6},{5,7},{6,0},{7,1},{8,10},{9,11},{10,... | collective-permute-start | bytes 393224 | tf_op jit(solution)/shard_map/ppermute | solution.py:30
  10.2 8.2 %collective-permute-start.2 = (f32[2,32,512]{2,1,0:T(8,128)S(1)}, f32[2,32,512]{2,1,0:T(8,128)S(1)}, u32[]{:S(2)}, u32[]{:S(2)}) collective-permute-start(f32[2,32,512]{2,1,0:T(8,128)S(1)} %pad_maximum_fusion), channel_id=1, source_target_pairs={{0,4},{1,5},{2,6},{3,7},{4,0},{5,1},{6,2},{7,3},{8,12},{9,13},{10,... | collective-permute-start | bytes 393224 | tf_op jit(solution)/shard_map/ppermute | solution.py:30
  12.7 6.1 %collective-permute-start.1 = (f32[2,32,512]{2,1,0:T(8,128)S(1)}, f32[2,32,512]{2,1,0:T(8,128)S(1)}, u32[]{:S(2)}, u32[]{:S(2)}) collective-permute-start(f32[2,32,512]{2,1,0:T(8,128)S(1)} %pad_maximum_fusion), channel_id=1, source_target_pairs={{0,6},{1,7},{2,0},{3,1},{4,2},{5,3},{6,4},{7,5},{8,14},{9,15},{10,... | collective-permute-start | bytes 393224 | tf_op jit(solution)/shard_map/ppermute | solution.py:30
  14.1 10.7 %collective-permute-start.7 = (f32[32,1024]{1,0:T(8,128)S(1)}, f32[32,1024]{1,0:T(8,128)S(1)}, u32[]{:S(2)}, u32[]{:S(2)}) collective-permute-start(f32[32,1024]{1,0:T(8,128)S(1)} %add.69), channel_id=1, source_target_pairs={{0,2},{1,3},{2,4},{3,5},{4,6},{5,7},{6,0},{7,1},{8,10},{9,11},{10,... | collective-permute-start | bytes 393224 | tf_op jit(solution)/shard_map/ppermute | solution.py:30
  15.0 9.8 %collective-permute-start.6 = (f32[32,1024]{1,0:T(8,128)S(1)}, f32[32,1024]{1,0:T(8,128)S(1)}, u32[]{:S(2)}, u32[]{:S(2)}) collective-permute-start(f32[32,1024]{1,0:T(8,128)S(1)} %add.69), channel_id=1, source_target_pairs={{0,6},{1,7},{2,0},{3,1},{4,2},{5,3},{6,4},{7,5},{8,14},{9,15},{10,... | collective-permute-start | bytes 393224 | tf_op jit(solution)/shard_map/ppermute | solution.py:30
  16.8 7.9 %collective-permute-start.5 = (f32[32,1024]{1,0:T(8,128)S(1)}, f32[32,1024]{1,0:T(8,128)}, u32[]{:S(2)}, u32[]{:S(2)}) collective-permute-start(f32[32,1024]{1,0:T(8,128)S(1)} %add.69), channel_id=1, source_target_pairs={{0,4},{1,5},{2,6},{3,7},{4,0},{5,1},{6,2},{7,3},{8,12},{9,13},{10,... | collective-permute-start | bytes 393224 | tf_op jit(solution)/shard_map/ppermute | solution.py:30
